TPU v7x, 256 devices: a whole 4x4x8 slice. The times are simulated.
256 devices in a mesh: frame: 32 (over z_lo, x, core), tile: 8 (over y, z_hi).
Axes of the slice: x: 4, y: 4, z: 8 (z_hi: 2, z_lo: 4; z = z_hi * 4 + z_lo), core: 2. Of those that a mesh axis runs over, the one named last changes fastest.
Arguments:
- queries: bfloat16 [32, 8, 64, 5120], P('frame', 'tile'), may hold values from -6 to 6
- keys: bfloat16 [32, 8, 64, 5120], P('frame', 'tile'), may hold values from -6 to 6
- values: bfloat16 [32, 8, 64, 5120], P('frame', 'tile'), may hold values from -6 to 6
- step_index: int32 [32], P('frame'), may hold values from 0 to 3
- frame_index: int32 [32], P('frame'), may hold values from 0 to 9
- window_mask: int32 [40, 9], replicated, may hold values 0 or 1
- history_mask: int32 [32, 5], P('frame'), may hold values 0 or 1
- step_gain: float32 [4, 40], replicated, may hold values from 0.5 to 2
Outputs:
- output: bfloat16 [32, 8, 64, 5120], P('frame', 'tile')
All inputs are finite; a program needn't handle non-finite values. No bound on the sum of `history_mask` on one device may be relied on, other than what follows from the above.
Results may differ from a plain program's by a relative error of at most 0.0095.
Values may be sent and summed in bfloat16 or wider, within the bound.
A program may use at most 128 MiB of HBM per device.

v0:
```python
import functools
import math

import jax
import jax.numpy as jnp
from jax import lax
from jax.experimental import pallas as pl
from jax.experimental.pallas import tpu as pltpu
from jax.sharding import PartitionSpec as P

HEADS = 40
HD = 128
TH = 8
TW = 8
BLK = 4
WIN = 5
STEPS = 4
CHUNK = 256

NEG_BIG = -1e30
MESH_ID = pl.DeviceIdType.MESH


def window_allowed(tile_count, tile_tok, head_masks, anchor):
    tile_cols = min(tile_count, 4)
    positions = jnp.arange(tile_count * tile_tok, dtype=jnp.int32) + anchor
    tile_of = positions // tile_tok
    within = positions % tile_tok
    row = tile_of // tile_cols * TH + within // TW
    col = tile_of % tile_cols * TW + within % TW
    row_step = row[None, :] // BLK - row[:, None] // BLK
    across = col[None, :] // BLK - col[:, None] // BLK
    nearby = (jnp.abs(row_step) <= 1) & (jnp.abs(across) <= 1)
    code = jnp.where(nearby, (row_step + 1) * 3 + across + 1, -1)
    allowed = (code == 4)[None]
    for offset in range(9):
        allowed = allowed | ((code == offset)[None] & (head_masks[:, offset] == 1)[:, None, None])
    return allowed


def relay_kernel(frames, use_ref, gain_ref, q_ref, kv_ref, mask_ref, out_ref,
                 slots, m_scr, l_scr, acc_scr, send_sem, recv_sem):
    me = lax.axis_index("frame")
    tile = lax.axis_index("tile")
    right = lax.rem(me + 1, frames)
    left = lax.rem(me + frames - 1, frames)
    head_share = acc_scr.shape[0]
    frame_tok = q_ref.shape[0]
    scale = 1.0 / math.sqrt(HD)

    barrier = pltpu.get_barrier_semaphore()
    for other in (left, right):
        pl.semaphore_signal(barrier, inc=1, device_id=(other, tile), device_id_type=MESH_ID)
    pl.semaphore_wait(barrier, 2)

    def copy_for(step):
        source = kv_ref if step == 0 else slots.at[step - 1]
        return pltpu.make_async_remote_copy(
            src_ref=source,
            dst_ref=slots.at[step],
            send_sem=send_sem.at[step],
            recv_sem=recv_sem.at[step],
            device_id=(right, tile),
            device_id_type=MESH_ID,
        )

    copies = [copy_for(step) for step in range(WIN)]

    @pl.when(me < frames - 1)
    def _():
        copies[0].start()

    m_scr[...] = jnp.full(m_scr.shape, NEG_BIG, jnp.float32)
    l_scr[...] = jnp.zeros(l_scr.shape, jnp.float32)
    acc_scr[...] = jnp.zeros(acc_scr.shape, jnp.float32)

    def attend(block, use):
        def head_body(h, carry):
            col = pl.multiple_of(h * HD, HD)
            key_h = block[0, :, pl.ds(col, HD)]
            value_h = block[1, :, pl.ds(col, HD)]
            for c in range(frame_tok // CHUNK):
                rows = pl.ds(c * CHUNK, CHUNK)
                query_h = q_ref[rows, pl.ds(col, HD)]
                scores = lax.dot_general(
                    query_h, key_h, (((1,), (1,)), ((), ())),
                    preferred_element_type=jnp.float32,
                ) * scale
                if use is None:
                    allowed = mask_ref[h, rows, :] > 0
                else:
                    allowed = jnp.broadcast_to(use > 0, scores.shape)
                scores = jnp.where(allowed, scores, NEG_BIG)
                old_max = m_scr[h, rows, :]
                new_max = jnp.maximum(old_max, jnp.max(scores, axis=1, keepdims=True))
                weights = jnp.where(allowed, jnp.exp(scores - new_max), 0.0)
                factor = jnp.exp(old_max - new_max)
                l_scr[h, rows, :] = l_scr[h, rows, :] * factor + jnp.sum(weights, axis=1, keepdims=True)
                acc_scr[h, rows, :] = acc_scr[h, rows, :] * factor + jnp.dot(
                    weights.astype(jnp.bfloat16), value_h, preferred_element_type=jnp.float32
                )
                m_scr[h, rows, :] = new_max
            return carry

        lax.fori_loop(0, head_share, head_body, 0)

    attend(kv_ref, None)
    for step in range(1, WIN + 1):
        @pl.when(me >= step)
        def _():
            copies[step - 1].wait_recv()
            if step < WIN:
                @pl.when(me < frames - 1)
                def _():
                    copies[step].start()
            attend(slots.at[step - 1], use_ref[step - 1])

    for step in range(WIN):
        @pl.when((me < frames - 1) & (me >= step))
        def _():
            copies[step].wait_send()

    def finish(h, carry):
        col = pl.multiple_of(h * HD, HD)
        out_ref[:, pl.ds(col, HD)] = (
            acc_scr[h] / l_scr[h] * gain_ref[h]
        ).astype(out_ref.dtype)
        return carry

    lax.fori_loop(0, head_share, finish, 0)


def relay_attend(frames, use, gains, q, kv, mask):
    head_share = gains.shape[0]
    frame_tok = q.shape[0]
    flops = 4 * (WIN + 1) * frame_tok * frame_tok * q.shape[1]
    smem = pl.BlockSpec(memory_space=pltpu.SMEM)
    vmem = pl.BlockSpec(memory_space=pltpu.VMEM)
    return pl.pallas_call(
        functools.partial(relay_kernel, frames),
        out_shape=jax.ShapeDtypeStruct(q.shape, jnp.bfloat16),
        in_specs=[smem, smem, vmem, vmem, vmem],
        out_specs=vmem,
        scratch_shapes=[
            pltpu.VMEM((WIN,) + kv.shape, kv.dtype),
            pltpu.VMEM((head_share, frame_tok, 1), jnp.float32),
            pltpu.VMEM((head_share, frame_tok, 1), jnp.float32),
            pltpu.VMEM((head_share, frame_tok, HD), jnp.float32),
            pltpu.SemaphoreType.DMA((WIN,)),
            pltpu.SemaphoreType.DMA((WIN,)),
        ],
        compiler_params=pltpu.CompilerParams(
            collective_id=0, has_side_effects=True, vmem_limit_bytes=48 * 1024 * 1024
        ),
        cost_estimate=pl.CostEstimate(
            flops=flops,
            transcendentals=(WIN + 1) * head_share * frame_tok * frame_tok,
            bytes_accessed=(WIN + 2) * kv.size * 2,
        ),
    )(use, gains, q, kv, mask)


def shards(queries, keys, values, step_index, frame_index, window_mask, history_mask, step_gain):
    tile_count = lax.axis_size("tile")
    frames = lax.axis_size("frame")
    tile_id = lax.axis_index("tile")
    group_id = lax.axis_index("frame")
    channels = queries.shape[-1]
    head_share = HEADS // tile_count
    tile_tok = queries.shape[2]
    frame_tok = tile_tok * tile_count
    picker = (jnp.arange(STEPS, dtype=jnp.int32) == step_index[0]).astype(jnp.float32)
    head_gains = jnp.dot(picker, step_gain, precision=lax.Precision.HIGHEST)
    my_gains = lax.dynamic_slice_in_dim(head_gains, tile_id * head_share, head_share)
    my_masks = lax.dynamic_slice_in_dim(window_mask, tile_id * head_share, head_share, axis=0)
    distance = jnp.arange(1, WIN + 1, dtype=jnp.int32)
    use = (
        (history_mask[0] == 1) & (distance <= frame_index[0]) & (group_id - distance >= 0)
    ).astype(jnp.int32)
    kv = lax.all_to_all(
        jnp.stack([keys[0, 0], values[0, 0]]), "tile", split_axis=2, concat_axis=1, tiled=True
    )
    q = lax.all_to_all(queries[0, 0], "tile", split_axis=1, concat_axis=0, tiled=True)
    anchor = jnp.minimum(step_index[0], 0) * 0
    mask = window_allowed(tile_count, tile_tok, my_masks, anchor).astype(jnp.bfloat16)
    finished = relay_attend(frames, use, my_gains, q, kv, mask)
    out = lax.all_to_all(finished, "tile", split_axis=0, concat_axis=1, tiled=True)
    return out.reshape(1, 1, tile_tok, channels)


def solution(mesh):
    return jax.shard_map(
        shards,
        mesh=mesh,
        in_specs=(
            P("frame", "tile", None, None),
            P("frame", "tile", None, None),
            P("frame", "tile", None, None),
            P("frame"),
            P("frame"),
            P(),
            P("frame", None),
            P(),
        ),
        out_specs=P("frame", "tile", None, None),
        check_vma=False,
    )
```

profile of v0, /device:TPU:32, one launch (start us, length us, event | category | flops | bytes accessed | tf_op | source)
XLA Modules:
  0.0 189.6 jit_solution(10814021421476375251)
XLA Ops:
  0.0 0.0 copy-start
  0.0 2.5 %pad_maximum_fusion = bf16[2,64,5120]{2,1,0:T(8,128)(2,1)} fusion(bf16[1,64,5120]{2,1,0:T(8,128)(2,1)} %bitcast.58, bf16[1,64,5120]{2,1,0:T(8,128)(2,1)} %bitcast.59), kind=kLoop, calls=%fused_computation.5 | loop fusion | flops 655360 | bytes 2621440 | tf_op jit(solution)/shard_map/stack | solution.py:181
  2.5 4.8 %copy.18 = bf16[2,64,5120]{1,0,2:T(2,128)(2,1)S(1)} copy(bf16[2,64,5120]{2,1,0:T(8,128)(2,1)} %pad_maximum_fusion) | data formatting | bytes 2621440 | tf_op jit(solution)/shard_map/stack | solution.py:181
  7.3 3.0 %reshape.856 = bf16[8,2,40960]{2,1,0:T(2,128)(2,1)} reshape(bf16[5120,2,64]{2,1,0:T(2,128)(2,1)S(1)} %bitcast.54) | data formatting | bytes 2621440
  10.4 0.0 copy-start.3
  10.4 10.3 %all-to-all-start.1 = ((bf16[8,2,40960]{2,1,0:T(2,128)(2,1)}), bf16[8,2,40960]{2,1,0:T(2,128)(2,1)S(1)}, u32[]{:S(2)}, u32[]{:S(2)}) async-start(bf16[8,2,40960]{2,1,0:T(2,128)(2,1)} %reshape.856), calls=%async_computation.1 | async-start | bytes 2621440 | tf_op jit(solution)/shard_map/all_to_all | solution.py:180
  21.3 0.0 copy-done.3
  21.3 0.0 copy-start.4
  21.4 0.1 copy.21
  21.4 0.9 copy.17
  22.4 0.0 copy-done.4
  22.4 0.7 compare_bitcast_fusion.8
  23.1 0.0 copy-start.5
  23.1 5.5 %broadcast_compare_fusion.6 = (pred[512,512]{1,0:T(8,128)(4,1)S(1)}, pred[512,512]{1,0:T(8,128)(4,1)}, pred[512,512]{1,0:T(8,128)(4,1)}, pred[512,512]{1,0:T(8,1...) fusion(s32[512]{0:T(512)S(1)} %get-tuple-element.23, ...), kind=kLoop, calls=%fused_computation.19 | loop fusion | flops 5505024 | bytes 2363392 | tf_op jit(solution)/shard_map/eq | solution.py:35
  28.6 28.6 %all-to-all-done.1 = bf16[8,2,40960]{2,1,0:T(2,128)(2,1)S(1)} async-done(((bf16[8,2,40960]{2,1,0:T(2,128)(2,1)}), bf16[8,2,40960]{2,1,0:T(2,128)(2,1)S(1)}, u32[]{:S(2)}, u32[]{:S(2)}) %all-to-all-start.1) | async-done | bytes 1310752 | tf_op jit(solution)/shard_map/all_to_all | solution.py:180
  57.2 0.0 copy-start.2
  57.2 1.1 copy-done.2
  58.3 3.5 %all-to-all-start = ((bf16[64,8,640]{2,0,1:T(8,128)(2,1)}), bf16[64,8,640]{2,0,1:T(8,128)(2,1)S(1)}, u32[]{:S(2)}, u32[]{:S(2)}) async-start(bf16[64,8,640]{2,0,1:T(8,128)(2,1)} %copy.17), calls=%async_computation | async-start | bytes 1310720 | tf_op jit(solution)/shard_map/all_to_all | solution.py:183
  61.9 0.0 copy-done
  61.9 0.1 convolution_bitcast_fusion
  62.0 0.1 dynamic_slice.6.gain_ref
  62.7 0.0 copy-done.5
  62.8 5.2 %or_convert_fusion.mask_ref = bf16[5,512,512]{2,1,0:T(8,128)(2,1)S(1)} fusion(pred[512,512]{1,0:T(8,128)(4,1)} %get-tuple-element.22, pred[512,512]{1,0:T(8,128)(4,1)} %get-tuple-element.21, pred[512,512]{1,0:T(8,128)(4,1)} %get-tuple-element.20, pred[512,512]{1,0:T(8,128)(4,1)} %get-tuple-element.19, pred[512,512]{1,0:T(8,128)(4,1)} %get-tuple-element.18, ...), kind=kLoop, calls=%fused_computation | loop fusion | flops 24903680 | bytes 4980781 | tf_op jit(solution)/shard_map/convert_element_type | solution.py:185
  68.0 4.6 %reshape.857 = bf16[5120,2,64]{2,1,0:T(2,128)(2,1)} reshape(bf16[8,2,40960]{2,1,0:T(2,128)(2,1)} %copy-done.2) | data formatting | bytes 2621440
  72.6 6.2 %copy.19 = bf16[2,64,8,640]{3,1,2,0:T(8,128)(2,1)} copy(bf16[2,64,8,640]{1,0,3,2:T(2,128)(2,1)} %bitcast.55) | data formatting | bytes 2621440 | tf_op jit(solution)/shard_map/all_to_all | solution.py:180
  78.7 0.7 all-to-all-done
  79.4 0.0 copy-start.1
  79.4 1.3 copy-done.1
  80.8 81.8 %shard_map.82 = bf16[512,640]{1,0:T(8,128)(2,1)S(1)} custom-call(s32[5]{0:T(128)S(1)} %fusion.28.use_ref, f32[5]{0:T(128)S(1)} %dynamic_slice.6.gain_ref, bf16[512,640]{1,0:T(8,128)(2,1)S(1)} %bitcast.52, bf16[2,512,640]{2,1,0:T(8,128)(2,1)S(1)} %bitcast.51, bf16[5,512,512]{2,1,0:T(8,128)(2,1)S(1)} %or_convert_fusion.mask_ref), custom_call_target="tpu_custom_call" | custom-call | flops 4026531840 | bytes 9175040 | tf_op jit(solution)/shard_map/pallas_call | solution.py:139
  162.6 25.5 %all_to_all.53 = bf16[8,64,640]{2,1,0:T(8,128)(2,1)S(1)} all-to-all(bf16[8,64,640]{2,1,0:T(8,128)(2,1)S(1)} %bitcast.53), channel_id=1, replica_groups=mesh['frame'=32,'tile'=8] {'tile'}, dimensions={0} | all-to-all | bytes 1310720 | tf_op jit(solution)/shard_map/all_to_all | solution.py:187
  188.1 0.4 copy.20
  188.5 1.1 reshape.853
  (2 shorter events, 0.0 us)
Async XLA Ops:
  0.0 61.9 %copy-start = (f32[4,40]{1,0:T(4,128)S(1)}, f32[4,40]{1,0:T(4,128)}, u32[]{:S(2)}) copy-start(f32[4,40]{1,0:T(4,128)} %param.15) | copy-start | bytes 1924
  10.4 11.0 %copy-start.3 = (bf16[1,1,64,5120]{3,2,1,0:T(8,128)(2,1)S(1)}, bf16[1,1,64,5120]{3,2,1,0:T(8,128)(2,1)}, u32[]{:S(2)}) copy-start(bf16[1,1,64,5120]{3,2,1,0:T(8,128)(2,1)} %param.8) | copy-start | bytes 1966084
  10.4 46.9 %all-to-all-start.1 = ((bf16[8,2,40960]{2,1,0:T(2,128)(2,1)}), bf16[8,2,40960]{2,1,0:T(2,128)(2,1)S(1)}, u32[]{:S(2)}, u32[]{:S(2)}) async-start(bf16[8,2,40960]{2,1,0:T(2,128)(2,1)} %reshape.856), calls=%async_computation.1 | async-start | bytes 2621440 | tf_op jit(solution)/shard_map/all_to_all | solution.py:180
  21.3 1.0 copy-start.4
  23.1 39.6 %copy-start.5 = (s32[1,5]{1,0:T(1,128)S(1)}, s32[1,5]{1,0:T(1,128)}, u32[]{:S(2)}) copy-start(s32[1,5]{1,0:T(1,128)} %param.14) | copy-start | bytes 64
  57.2 1.1 copy-start.2
  58.3 21.1 %all-to-all-start = ((bf16[64,8,640]{2,0,1:T(8,128)(2,1)}), bf16[64,8,640]{2,0,1:T(8,128)(2,1)S(1)}, u32[]{:S(2)}, u32[]{:S(2)}) async-start(bf16[64,8,640]{2,0,1:T(8,128)(2,1)} %copy.17), calls=%async_computation | async-start | bytes 1310720 | tf_op jit(solution)/shard_map/all_to_all | solution.py:183
  79.4 1.3 copy-start.1
where the time goes:
time: 190 us
  Pallas kernels  81.8 us (43%)
  waiting for transfers between devices  29.3 us (15%)
  blocking collectives  25.5 us (13%)
  local copies, waits for them, and re-layouts  23.6 us (12%)
  other arithmetic  14 us (7%)
  starting transfers between devices  13.9 us (7%)
    pallas_call x1, Pallas kernels, relay_attend(): pl.pallas_call(functools.partial(relay_kernel, frames), out_shape=jax.Sha...  81.8 us
    all_to_all x1, waiting for transfers between devices, shards(): lax.all_to_all(jnp.stack([keys[0, 0], values[0, 0]]), 'tile', split_axis=...  28.6 us
    all_to_all x1, blocking collectives, shards(): lax.all_to_all(finished, 'tile', split_axis=0, concat_axis=1, tiled=True)  25.5 us
    all_to_all x1, starting transfers between devices, shards(): lax.all_to_all(jnp.stack([keys[0, 0], values[0, 0]]), 'tile', split_axis=...  10.3 us
    unnamed x15, local copies, waits for them, and re-layouts  10.1 us
    all_to_all x1, local copies, waits for them, and re-layouts, shards(): lax.all_to_all(jnp.stack([keys[0, 0], values[0, 0]]), 'tile', split_axis=...  6.16 us
    eq x1, other arithmetic, window_allowed(): allowed = (code == 4)[None]  5.54 us
    convert_element_type x1, other arithmetic, shards(): window_allowed(tile_count, tile_tok, my_masks, anchor).astype(jnp.bfloat16)  5.19 us
  transfers between devices with their start and end apart: 2, of which 2 were waited for; matrix products, arithmetic and copies ran while one was open for 12% of the time, Pallas kernels for 0%

commit v1 on v0

--- a/solution.py
+++ b/solution.py
@@ -38,23 +38,78 @@
     return allowed
 
 
-def relay_kernel(frames, use_ref, gain_ref, q_ref, kv_ref, mask_ref, out_ref,
-                 slots, m_scr, l_scr, acc_scr, send_sem, recv_sem):
+def fused_kernel(frames, tiles, use_ref, gain_ref, q_ref, k_ref, v_ref, mask_ref, out_ref,
+                 own_kv, own_q, slots, fin, got_out, m_scr, l_scr, acc_scr,
+                 piece_send, piece_recv, local_sem, send_sem, recv_sem):
     me = lax.axis_index("frame")
     tile = lax.axis_index("tile")
     right = lax.rem(me + 1, frames)
     left = lax.rem(me + frames - 1, frames)
     head_share = acc_scr.shape[0]
-    frame_tok = q_ref.shape[0]
+    frame_tok = own_q.shape[0]
+    share = own_q.shape[1]
+    tile_tok = q_ref.shape[0]
     scale = 1.0 / math.sqrt(HD)
 
     barrier = pltpu.get_barrier_semaphore()
     for other in (left, right):
         pl.semaphore_signal(barrier, inc=1, device_id=(other, tile), device_id_type=MESH_ID)
-    pl.semaphore_wait(barrier, 2)
+    for offset in range(1, tiles):
+        peer = lax.rem(tile + offset, tiles)
+        pl.semaphore_signal(barrier, inc=1, device_id=(me, peer), device_id_type=MESH_ID)
+    pl.semaphore_wait(barrier, 2 + tiles - 1)
+
+    def channels_of(p):
+        return pl.ds(pl.multiple_of(p * share, 128), share)
+
+    def tokens_of(p):
+        return pl.ds(pl.multiple_of(p * tile_tok, tile_tok), tile_tok)
+
+    sources = [k_ref, v_ref, q_ref]
+    targets = [lambda rows: own_kv.at[0, rows, :], lambda rows: own_kv.at[1, rows, :],
+               lambda rows: own_q.at[rows, :]]
+
+    def piece_out(which, offset):
+        peer = lax.rem(tile + offset, tiles)
+        return pltpu.make_async_remote_copy(
+            src_ref=sources[which].at[:, channels_of(peer)],
+            dst_ref=targets[which](tokens_of(tile)),
+            send_sem=piece_send.at[which, offset],
+            recv_sem=piece_recv.at[which, tile],
+            device_id=(me, peer),
+            device_id_type=MESH_ID,
+        )
+
+    def piece_in(which, offset):
+        sender = lax.rem(tile + tiles - offset, tiles)
+        return pltpu.make_async_remote_copy(
+            src_ref=sources[which].at[:, channels_of(tile)],
+            dst_ref=targets[which](tokens_of(sender)),
+            send_sem=piece_send.at[which, offset],
+            recv_sem=piece_recv.at[which, sender],
+            device_id=(me, sender),
+            device_id_type=MESH_ID,
+        )
+
+    locals_ = [
+        pltpu.make_async_copy(
+            sources[which].at[:, channels_of(tile)], targets[which](tokens_of(tile)),
+            local_sem.at[which],
+        )
+        for which in range(3)
+    ]
+    for which in range(3):
+        locals_[which].start()
+        for offset in range(1, tiles):
+            piece_out(which, offset).start()
+
+    for which in range(2):
+        locals_[which].wait()
+        for offset in range(1, tiles):
+            piece_in(which, offset).wait_recv()
 
     def copy_for(step):
-        source = kv_ref if step == 0 else slots.at[step - 1]
+        source = own_kv if step == 0 else slots.at[step - 1]
         return pltpu.make_async_remote_copy(
             src_ref=source,
             dst_ref=slots.at[step],
@@ -73,6 +128,10 @@
     m_scr[...] = jnp.full(m_scr.shape, NEG_BIG, jnp.float32)
     l_scr[...] = jnp.zeros(l_scr.shape, jnp.float32)
     acc_scr[...] = jnp.zeros(acc_scr.shape, jnp.float32)
+
+    locals_[2].wait()
+    for offset in range(1, tiles):
+        piece_in(2, offset).wait_recv()
 
     def attend(block, use):
         def head_body(h, carry):
@@ -81,7 +140,7 @@
             value_h = block[1, :, pl.ds(col, HD)]
             for c in range(frame_tok // CHUNK):
                 rows = pl.ds(c * CHUNK, CHUNK)
-                query_h = q_ref[rows, pl.ds(col, HD)]
+                query_h = own_q[rows, pl.ds(col, HD)]
                 scores = lax.dot_general(
                     query_h, key_h, (((1,), (1,)), ((), ())),
                     preferred_element_type=jnp.float32,
@@ -104,7 +163,7 @@
 
         lax.fori_loop(0, head_share, head_body, 0)
 
-    attend(kv_ref, None)
+    attend(own_kv, None)
     for step in range(1, WIN + 1):
         @pl.when(me >= step)
         def _():
@@ -115,49 +174,93 @@
                     copies[step].start()
             attend(slots.at[step - 1], use_ref[step - 1])
 
+    def finish(h, carry):
+        col = pl.multiple_of(h * HD, HD)
+        fin[:, pl.ds(col, HD)] = (acc_scr[h] / l_scr[h] * gain_ref[h]).astype(fin.dtype)
+        return carry
+
+    lax.fori_loop(0, head_share, finish, 0)
+
+    def back_out(offset):
+        peer = lax.rem(tile + offset, tiles)
+        return pltpu.make_async_remote_copy(
+            src_ref=fin.at[tokens_of(peer), :],
+            dst_ref=got_out.at[:, channels_of(tile)],
+            send_sem=piece_send.at[3, offset],
+            recv_sem=piece_recv.at[3, tile],
+            device_id=(me, peer),
+            device_id_type=MESH_ID,
+        )
+
+    def back_in(offset):
+        sender = lax.rem(tile + tiles - offset, tiles)
+        return pltpu.make_async_remote_copy(
+            src_ref=fin.at[tokens_of(tile), :],
+            dst_ref=got_out.at[:, channels_of(sender)],
+            send_sem=piece_send.at[3, offset],
+            recv_sem=piece_recv.at[3, sender],
+            device_id=(me, sender),
+            device_id_type=MESH_ID,
+        )
+
+    home = pltpu.make_async_copy(fin.at[tokens_of(tile), :], got_out.at[:, channels_of(tile)],
+                                 local_sem.at[3])
+    home.start()
+    for offset in range(1, tiles):
+        back_out(offset).start()
+    home.wait()
+    for offset in range(1, tiles):
+        back_in(offset).wait_recv()
+    out_ref[...] = got_out[...]
+
+    for which in range(3):
+        for offset in range(1, tiles):
+            piece_out(which, offset).wait_send()
+    for offset in range(1, tiles):
+        back_out(offset).wait_send()
     for step in range(WIN):
         @pl.when((me < frames - 1) & (me >= step))
         def _():
             copies[step].wait_send()
 
-    def finish(h, carry):
-        col = pl.multiple_of(h * HD, HD)
-        out_ref[:, pl.ds(col, HD)] = (
-            acc_scr[h] / l_scr[h] * gain_ref[h]
-        ).astype(out_ref.dtype)
-        return carry
-
-    lax.fori_loop(0, head_share, finish, 0)
-
-
-def relay_attend(frames, use, gains, q, kv, mask):
+
+def fused_attend(frames, tiles, use, gains, q, k, v, mask):
     head_share = gains.shape[0]
-    frame_tok = q.shape[0]
-    flops = 4 * (WIN + 1) * frame_tok * frame_tok * q.shape[1]
+    tile_tok, channels = q.shape
+    frame_tok = tile_tok * tiles
+    share = channels // tiles
+    flops = 4 * (WIN + 1) * frame_tok * frame_tok * share
     smem = pl.BlockSpec(memory_space=pltpu.SMEM)
     vmem = pl.BlockSpec(memory_space=pltpu.VMEM)
     return pl.pallas_call(
-        functools.partial(relay_kernel, frames),
+        functools.partial(fused_kernel, frames, tiles),
         out_shape=jax.ShapeDtypeStruct(q.shape, jnp.bfloat16),
-        in_specs=[smem, smem, vmem, vmem, vmem],
+        in_specs=[smem, smem, vmem, vmem, vmem, vmem],
         out_specs=vmem,
         scratch_shapes=[
-            pltpu.VMEM((WIN,) + kv.shape, kv.dtype),
+            pltpu.VMEM((2, frame_tok, share), jnp.bfloat16),
+            pltpu.VMEM((frame_tok, share), jnp.bfloat16),
+            pltpu.VMEM((WIN, 2, frame_tok, share), jnp.bfloat16),
+            pltpu.VMEM((frame_tok, share), jnp.bfloat16),
+            pltpu.VMEM((tile_tok, channels), jnp.bfloat16),
             pltpu.VMEM((head_share, frame_tok, 1), jnp.float32),
             pltpu.VMEM((head_share, frame_tok, 1), jnp.float32),
             pltpu.VMEM((head_share, frame_tok, HD), jnp.float32),
+            pltpu.SemaphoreType.DMA((4, tiles)),
+            pltpu.SemaphoreType.DMA((4, tiles)),
+            pltpu.SemaphoreType.DMA((4,)),
             pltpu.SemaphoreType.DMA((WIN,)),
             pltpu.SemaphoreType.DMA((WIN,)),
         ],
         compiler_params=pltpu.CompilerParams(
-            collective_id=0, has_side_effects=True, vmem_limit_bytes=48 * 1024 * 1024
+            collective_id=0, has_side_effects=True, vmem_limit_bytes=56 * 1024 * 1024
         ),
         cost_estimate=pl.CostEstimate(
             flops=flops,
             transcendentals=(WIN + 1) * head_share * frame_tok * frame_tok,
-            bytes_accessed=(WIN + 2) * kv.size * 2,
+            bytes_accessed=(WIN + 6) * 2 * frame_tok * share * 2,
         ),
-    )(use, gains, q, kv, mask)
+    )(use, gains, q, k, v, mask)
 
 
 def shards(queries, keys, values, step_index, frame_index, window_mask, history_mask, step_gain):
@@ -177,15 +280,12 @@
     use = (
         (history_mask[0] == 1) & (distance <= frame_index[0]) & (group_id - distance >= 0)
     ).astype(jnp.int32)
-    kv = lax.all_to_all(
-        jnp.stack([keys[0, 0], values[0, 0]]), "tile", split_axis=2, concat_axis=1, tiled=True
-    )
-    q = lax.all_to_all(queries[0, 0], "tile", split_axis=1, concat_axis=0, tiled=True)
     anchor = jnp.minimum(step_index[0], 0) * 0
     mask = window_allowed(tile_count, tile_tok, my_masks, anchor).astype(jnp.bfloat16)
-    finished = relay_attend(frames, use, my_gains, q, kv, mask)
-    out = lax.all_to_all(finished, "tile", split_axis=0, concat_axis=1, tiled=True)
-    return out.reshape(1, 1, tile_tok, channels)
+    finished = fused_attend(
+        frames, tile_count, use, my_gains, queries[0, 0], keys[0, 0], values[0, 0], mask
+    )
+    return finished.reshape(1, 1, tile_tok, channels)
 
 
 def solution(mesh):

time: 190 us -> 167 us (0.88)
  the two profiles are of different devices: /device:TPU:32 before, /device:TPU:192 now
where the time goes in v1:
time: 167 us
  Pallas kernels  154 us (92%)
  other arithmetic  9.43 us (6%)
  local copies, waits for them, and re-layouts  2.59 us (2%)
    pallas_call x1, Pallas kernels, fused_attend(): pl.pallas_call(functools.partial(fused_kernel, frames, tiles), out_shape=...  154 us
    convert_element_type x1, other arithmetic, shards(): window_allowed(tile_count, tile_tok, my_masks, anchor).astype(jnp.bfloat16)  4.9 us

profile of v1, /device:TPU:192, one launch (start us, length us, event | category | flops | bytes accessed | tf_op | source)
XLA Modules:
  0.0 167.2 jit_solution(6770494566631532535)
XLA Ops:
  0.0 0.0 copy-start
  1.3 0.0 copy-done
  1.3 0.1 convolution_bitcast_fusion
  1.4 0.6 dynamic_slice.6.gain_ref
  2.1 1.2 fusion.28.use_ref
  3.3 1.1 compare_bitcast_fusion.8
  4.4 2.2 %broadcast_compare_fusion.6 = (pred[512,512]{1,0:T(8,128)(4,1)S(1)}, pred[512,512]{1,0:T(8,128)(4,1)S(1)}, pred[512,512]{1,0:T(8,128)(4,1)S(1)}, pred[512,512]{1...) fusion(s32[512]{0:T(512)S(1)} %get-tuple-element.23, ...), kind=kLoop, calls=%fused_computation.18 | loop fusion | flops 5505024 | bytes 2363392 | tf_op jit(solution)/shard_map/eq | solution.py:35
  6.6 4.9 %or_convert_fusion.mask_ref = bf16[5,512,512]{2,1,0:T(8,128)(2,1)} fusion(pred[512,512]{1,0:T(8,128)(4,1)S(1)} %get-tuple-element.22, pred[512,512]{1,0:T(8,128)(4,1)S(1)} %get-tuple-element.21, pred[512,512]{1,0:T(8,128)(4,1)S(1)} %get-tuple-element.20, pred[512,512]{1,0:T(8,128)(4,1)S(1)} %get-tuple-element.19, pred[512,512]{1,0:T(8,128)(4,1)S(1)} %get-tuple-element.18, ...), kind=kLoop, calls=%fused_computation | loop fusion | flops 24903680 | bytes 4980781 | tf_op jit(solution)/shard_map/convert_element_type | solution.py:284
  11.5 153.8 %shard_map.82 = bf16[64,5120]{1,0:T(8,128)(2,1)} custom-call(s32[5]{0:T(128)} %fusion.28.use_ref, f32[5]{0:T(128)} %dynamic_slice.6.gain_ref, bf16[64,5120]{1,0:T(8,128)(2,1)} %bitcast.39, bf16[64,5120]{1,0:T(8,128)(2,1)} %bitcast.40, bf16[64,5120]{1,0:T(8,128)(2,1)} %bitcast.41, bf16[5,512,512]{2,1,0:T(8,128)(2,1)} %or_convert_fusion.mask_ref), custom_call_target="tpu_custom_call" | custom-call | flops 4026531840 | bytes 14417920 | tf_op jit(solution)/shard_map/pallas_call | solution.py:235
  165.3 2.0 %copy.12 = bf16[1,1,64,5120]{3,2,1,0:T(8,128)(2,1)} copy(bf16[1,1,64,5120]{3,2,1,0:T(8,128)(2,1)} %bitcast.38) | data formatting | bytes 1310720
  (1 shorter events, 0.0 us)
Async XLA Ops:
  0.0 1.3 copy-start

commit v2 on v1

--- a/solution.py
+++ b/solution.py
@@ -21,26 +21,18 @@
 MESH_ID = pl.DeviceIdType.MESH
 
 
-def window_allowed(tile_count, tile_tok, head_masks, anchor):
+def block_place(positions, tile_count, tile_tok):
     tile_cols = min(tile_count, 4)
-    positions = jnp.arange(tile_count * tile_tok, dtype=jnp.int32) + anchor
     tile_of = positions // tile_tok
     within = positions % tile_tok
     row = tile_of // tile_cols * TH + within // TW
     col = tile_of % tile_cols * TW + within % TW
-    row_step = row[None, :] // BLK - row[:, None] // BLK
-    across = col[None, :] // BLK - col[:, None] // BLK
-    nearby = (jnp.abs(row_step) <= 1) & (jnp.abs(across) <= 1)
-    code = jnp.where(nearby, (row_step + 1) * 3 + across + 1, -1)
-    allowed = (code == 4)[None]
-    for offset in range(9):
-        allowed = allowed | ((code == offset)[None] & (head_masks[:, offset] == 1)[:, None, None])
-    return allowed
-
-
-def fused_kernel(frames, tiles, use_ref, gain_ref, q_ref, k_ref, v_ref, mask_ref, out_ref,
-                 own_kv, own_q, slots, fin, got_out, m_scr, l_scr, acc_scr,
-                 piece_send, piece_recv, local_sem, send_sem, recv_sem):
+    return row // BLK, col // BLK
+
+
+def fused_kernel(frames, tiles, use_ref, gain_ref, bits_ref, q_ref, k_ref, v_ref, out_ref,
+                 own_kv, own_q, slots, fin, got_out, code_scr, m_scr, l_scr, acc_scr,
+                 piece_send, piece_recv, local_sem, send_sem, recv_sem, hop_send, hop_recv):
     me = lax.axis_index("frame")
     tile = lax.axis_index("tile")
     right = lax.rem(me + 1, frames)
@@ -98,15 +90,47 @@
         )
         for which in range(3)
     ]
+    far_first = [j for j in range(1, tiles) if j % 2] + [j for j in range(1, tiles) if j % 2 == 0]
+    near_first = far_first[::-1]
     for which in range(3):
         locals_[which].start()
-        for offset in range(1, tiles):
+        for offset in far_first:
             piece_out(which, offset).start()
+
+    for c in range(frame_tok // CHUNK):
+        query_pos = c * CHUNK + lax.broadcasted_iota(jnp.int32, (CHUNK, frame_tok), 0)
+        key_pos = lax.broadcasted_iota(jnp.int32, (CHUNK, frame_tok), 1)
+        query_row, query_col = block_place(query_pos, tiles, tile_tok)
+        key_row, key_col = block_place(key_pos, tiles, tile_tok)
+        row_step = key_row - query_row
+        across = key_col - query_col
+        nearby = (row_step >= -1) & (row_step <= 1) & (across >= -1) & (across <= 1)
+        code_scr[pl.ds(c * CHUNK, CHUNK), :] = jnp.where(nearby, (row_step + 1) * 3 + across + 1, 15)
+
+    def first_hop(p):
+        return pltpu.make_async_remote_copy(
+            src_ref=own_kv.at[:, tokens_of(p), :],
+            dst_ref=slots.at[0, :, tokens_of(p), :],
+            send_sem=hop_send.at[p],
+            recv_sem=hop_recv.at[p],
+            device_id=(right, tile),
+            device_id_type=MESH_ID,
+        )
 
     for which in range(2):
         locals_[which].wait()
-        for offset in range(1, tiles):
+
+    @pl.when(me < frames - 1)
+    def _():
+        first_hop(tile).start()
+
+    for offset in near_first:
+        for which in range(2):
             piece_in(which, offset).wait_recv()
+
+        @pl.when(me < frames - 1)
+        def _():
+            first_hop(lax.rem(tile + tiles - offset, tiles)).start()
 
     def copy_for(step):
         source = own_kv if step == 0 else slots.at[step - 1]
@@ -119,11 +143,7 @@
             device_id_type=MESH_ID,
         )
 
-    copies = [copy_for(step) for step in range(WIN)]
-
-    @pl.when(me < frames - 1)
-    def _():
-        copies[0].start()
+    copies = [None] + [copy_for(step) for step in range(1, WIN)]
 
     m_scr[...] = jnp.full(m_scr.shape, NEG_BIG, jnp.float32)
     l_scr[...] = jnp.zeros(l_scr.shape, jnp.float32)
@@ -146,7 +166,9 @@
                     preferred_element_type=jnp.float32,
                 ) * scale
                 if use is None:
-                    allowed = mask_ref[h, rows, :] > 0
+                    code = code_scr[rows, :]
+                    shifted = lax.shift_right_logical(jnp.broadcast_to(bits_ref[h], code.shape), code)
+                    allowed = (shifted & 1) == 1
                 else:
                     allowed = jnp.broadcast_to(use > 0, scores.shape)
                 scores = jnp.where(allowed, scores, NEG_BIG)
@@ -167,7 +189,11 @@
     for step in range(1, WIN + 1):
         @pl.when(me >= step)
         def _():
-            copies[step - 1].wait_recv()
+            if step == 1:
+                for p in range(tiles):
+                    first_hop(p).wait_recv()
+            else:
+                copies[step - 1].wait_recv()
             if step < WIN:
                 @pl.when(me < frames - 1)
                 def _():
@@ -218,13 +244,18 @@
             piece_out(which, offset).wait_send()
     for offset in range(1, tiles):
         back_out(offset).wait_send()
-    for step in range(WIN):
+    for step in range(1, WIN):
         @pl.when((me < frames - 1) & (me >= step))
         def _():
             copies[step].wait_send()
 
-
-def fused_attend(frames, tiles, use, gains, q, k, v, mask):
+    @pl.when(me < frames - 1)
+    def _():
+        for p in range(tiles):
+            first_hop(p).wait_send()
+
+
+def fused_attend(frames, tiles, use, gains, bits, q, k, v):
     head_share = gains.shape[0]
     tile_tok, channels = q.shape
     frame_tok = tile_tok * tiles
@@ -235,7 +266,7 @@
     return pl.pallas_call(
         functools.partial(fused_kernel, frames, tiles),
         out_shape=jax.ShapeDtypeStruct(q.shape, jnp.bfloat16),
-        in_specs=[smem, smem, vmem, vmem, vmem, vmem],
+        in_specs=[smem, smem, smem, vmem, vmem, vmem],
         out_specs=vmem,
         scratch_shapes=[
             pltpu.VMEM((2, frame_tok, share), jnp.bfloat16),
@@ -243,6 +274,7 @@
             pltpu.VMEM((WIN, 2, frame_tok, share), jnp.bfloat16),
             pltpu.VMEM((frame_tok, share), jnp.bfloat16),
             pltpu.VMEM((tile_tok, channels), jnp.bfloat16),
+            pltpu.VMEM((frame_tok, frame_tok), jnp.int32),
             pltpu.VMEM((head_share, frame_tok, 1), jnp.float32),
             pltpu.VMEM((head_share, frame_tok, 1), jnp.float32),
             pltpu.VMEM((head_share, frame_tok, HD), jnp.float32),
@@ -251,6 +283,8 @@
             pltpu.SemaphoreType.DMA((4,)),
             pltpu.SemaphoreType.DMA((WIN,)),
             pltpu.SemaphoreType.DMA((WIN,)),
+            pltpu.SemaphoreType.DMA((tiles,)),
+            pltpu.SemaphoreType.DMA((tiles,)),
         ],
         compiler_params=pltpu.CompilerParams(
             collective_id=0, has_side_effects=True, vmem_limit_bytes=56 * 1024 * 1024
@@ -260,7 +294,7 @@
             transcendentals=(WIN + 1) * head_share * frame_tok * frame_tok,
             bytes_accessed=(WIN + 6) * 2 * frame_tok * share * 2,
         ),
-    )(use, gains, q, k, v, mask)
+    )(use, gains, bits, q, k, v)
 
 
 def shards(queries, keys, values, step_index, frame_index, window_mask, history_mask, step_gain):
@@ -280,10 +314,12 @@
     use = (
         (history_mask[0] == 1) & (distance <= frame_index[0]) & (group_id - distance >= 0)
     ).astype(jnp.int32)
-    anchor = jnp.minimum(step_index[0], 0) * 0
-    mask = window_allowed(tile_count, tile_tok, my_masks, anchor).astype(jnp.bfloat16)
+    bits = jnp.sum(
+        jnp.where(my_masks == 1, jnp.left_shift(1, jnp.arange(9, dtype=jnp.int32)), 0), axis=1
+    ) | 16
     finished = fused_attend(
-        frames, tile_count, use, my_gains, queries[0, 0], keys[0, 0], values[0, 0], mask
+        frames, tile_count, use, my_gains, bits.astype(jnp.int32),
+        queries[0, 0], keys[0, 0], values[0, 0],
     )
     return finished.reshape(1, 1, tile_tok, channels)
 

time: 167 us -> 154 us (0.922)
  the two profiles are of different devices: /device:TPU:192 before, /device:TPU:224 now
where the time goes in v2:
time: 154 us
  Pallas kernels  149 us (97%)
  local copies, waits for them, and re-layouts  2.6 us (2%)
    pallas_call x1, Pallas kernels, fused_attend(): pl.pallas_call(functools.partial(fused_kernel, frames, tiles), out_shape=...  149 us

profile of v2, /device:TPU:224, one launch (start us, length us, event | category | flops | bytes accessed | tf_op | source)
XLA Modules:
  0.0 153.8 jit_solution(17486047186792886550)
XLA Ops:
  0.0 0.0 copy-start
  0.7 0.0 copy-start.2
  1.3 0.0 copy-start.1
  1.3 0.0 copy-done
  1.4 0.1 convolution_bitcast_fusion
  1.5 0.6 dynamic_slice.6.gain_ref
  2.1 0.0 copy-done.2
  2.1 0.6 fusion.2.use_ref
  2.7 0.0 copy-done.1
  2.7 0.1 select_reduce_fusion
  2.8 0.5 broadcast_or_fusion.bits_ref
  3.3 148.5 %shard_map.82 = bf16[64,5120]{1,0:T(8,128)(2,1)} custom-call(s32[5]{0:T(128)} %fusion.2.use_ref, f32[5]{0:T(128)} %dynamic_slice.6.gain_ref, s32[5]{0:T(128)} %broadcast_or_fusion.bits_ref, bf16[64,5120]{1,0:T(8,128)(2,1)} %bitcast.21, bf16[64,5120]{1,0:T(8,128)(2,1)} %bitcast.22, bf16[64,5120]{1,0:T(8,128)(2,1)} %bitcast.23), custom_call_target="tpu_custom_call" | custom-call | flops 4026531840 | bytes 14417920 | tf_op jit(solution)/shard_map/pallas_call | solution.py:266
  151.8 2.0 %copy.12 = bf16[1,1,64,5120]{3,2,1,0:T(8,128)(2,1)} copy(bf16[1,1,64,5120]{3,2,1,0:T(8,128)(2,1)} %bitcast.20) | data formatting | bytes 1310720
  (1 shorter events, 0.0 us)
Async XLA Ops:
  0.0 1.3 copy-start
  0.7 1.4 copy-start.2
  1.3 1.3 copy-start.1

commit v3 on v2

--- a/solution.py
+++ b/solution.py
@@ -32,7 +32,7 @@
 
 def fused_kernel(frames, tiles, use_ref, gain_ref, bits_ref, q_ref, k_ref, v_ref, out_ref,
                  own_kv, own_q, slots, fin, got_out, code_scr, m_scr, l_scr, acc_scr,
-                 piece_send, piece_recv, local_sem, send_sem, recv_sem, hop_send, hop_recv):
+                 piece_send, piece_recv, local_sem, hop_send, hop_recv):
     me = lax.axis_index("frame")
     tile = lax.axis_index("tile")
     right = lax.rem(me + 1, frames)
@@ -97,6 +97,46 @@
         for offset in far_first:
             piece_out(which, offset).start()
 
+    def hop(step, p):
+        source = own_kv if step == 0 else slots.at[step - 1]
+        return pltpu.make_async_remote_copy(
+            src_ref=source.at[:, tokens_of(p), :],
+            dst_ref=slots.at[step, :, tokens_of(p), :],
+            send_sem=hop_send.at[step, p],
+            recv_sem=hop_recv.at[step, p],
+            device_id=(right, tile),
+            device_id_type=MESH_ID,
+        )
+
+    def pass_on(step, p):
+        @pl.when((me < frames - 1) & (me >= step))
+        def _():
+            hop(step, p).start()
+
+    def take(step, p):
+        @pl.when(me >= step + 1)
+        def _():
+            hop(step, p).wait_recv()
+
+    def sender_of(offset):
+        return lax.rem(tile + tiles - offset, tiles)
+
+    early = [0] + [j for j in near_first if j % 2 == 0]
+    late = [j for j in range(1, tiles) if j % 2]
+
+    for which in range(2):
+        locals_[which].wait()
+    for offset in early:
+        p = sender_of(offset)
+        if offset:
+            for which in range(2):
+                piece_in(which, offset).wait_recv()
+        pass_on(0, p)
+        for step in range(1, WIN):
+            take(step - 1, p)
+            pass_on(step, p)
+        take(WIN - 1, p)
+
     for c in range(frame_tok // CHUNK):
         query_pos = c * CHUNK + lax.broadcasted_iota(jnp.int32, (CHUNK, frame_tok), 0)
         key_pos = lax.broadcasted_iota(jnp.int32, (CHUNK, frame_tok), 1)
@@ -106,48 +146,14 @@
         across = key_col - query_col
         nearby = (row_step >= -1) & (row_step <= 1) & (across >= -1) & (across <= 1)
         code_scr[pl.ds(c * CHUNK, CHUNK), :] = jnp.where(nearby, (row_step + 1) * 3 + across + 1, 15)
-
-    def first_hop(p):
-        return pltpu.make_async_remote_copy(
-            src_ref=own_kv.at[:, tokens_of(p), :],
-            dst_ref=slots.at[0, :, tokens_of(p), :],
-            send_sem=hop_send.at[p],
-            recv_sem=hop_recv.at[p],
-            device_id=(right, tile),
-            device_id_type=MESH_ID,
-        )
-
-    for which in range(2):
-        locals_[which].wait()
-
-    @pl.when(me < frames - 1)
-    def _():
-        first_hop(tile).start()
-
-    for offset in near_first:
-        for which in range(2):
-            piece_in(which, offset).wait_recv()
-
-        @pl.when(me < frames - 1)
-        def _():
-            first_hop(lax.rem(tile + tiles - offset, tiles)).start()
-
-    def copy_for(step):
-        source = own_kv if step == 0 else slots.at[step - 1]
-        return pltpu.make_async_remote_copy(
-            src_ref=source,
-            dst_ref=slots.at[step],
-            send_sem=send_sem.at[step],
-            recv_sem=recv_sem.at[step],
-            device_id=(right, tile),
-            device_id_type=MESH_ID,
-        )
-
-    copies = [None] + [copy_for(step) for step in range(1, WIN)]
-
     m_scr[...] = jnp.full(m_scr.shape, NEG_BIG, jnp.float32)
     l_scr[...] = jnp.zeros(l_scr.shape, jnp.float32)
     acc_scr[...] = jnp.zeros(acc_scr.shape, jnp.float32)
+
+    for offset in late:
+        for which in range(2):
+            piece_in(which, offset).wait_recv()
+        pass_on(0, sender_of(offset))
 
     locals_[2].wait()
     for offset in range(1, tiles):
@@ -168,13 +174,12 @@
                 if use is None:
                     code = code_scr[rows, :]
                     shifted = lax.shift_right_logical(jnp.broadcast_to(bits_ref[h], code.shape), code)
-                    allowed = (shifted & 1) == 1
+                    scores = jnp.where((shifted & 1) == 1, scores, NEG_BIG)
                 else:
-                    allowed = jnp.broadcast_to(use > 0, scores.shape)
-                scores = jnp.where(allowed, scores, NEG_BIG)
+                    scores = scores + jnp.where(use > 0, 0.0, NEG_BIG)
                 old_max = m_scr[h, rows, :]
                 new_max = jnp.maximum(old_max, jnp.max(scores, axis=1, keepdims=True))
-                weights = jnp.where(allowed, jnp.exp(scores - new_max), 0.0)
+                weights = jnp.exp(scores - new_max)
                 factor = jnp.exp(old_max - new_max)
                 l_scr[h, rows, :] = l_scr[h, rows, :] * factor + jnp.sum(weights, axis=1, keepdims=True)
                 acc_scr[h, rows, :] = acc_scr[h, rows, :] * factor + jnp.dot(
@@ -187,17 +192,13 @@
 
     attend(own_kv, None)
     for step in range(1, WIN + 1):
+        for offset in late:
+            take(step - 1, sender_of(offset))
+            if step < WIN:
+                pass_on(step, sender_of(offset))
+
         @pl.when(me >= step)
         def _():
-            if step == 1:
-                for p in range(tiles):
-                    first_hop(p).wait_recv()
-            else:
-                copies[step - 1].wait_recv()
-            if step < WIN:
-                @pl.when(me < frames - 1)
-                def _():
-                    copies[step].start()
             attend(slots.at[step - 1], use_ref[step - 1])
 
     def finish(h, carry):
@@ -244,15 +245,11 @@
             piece_out(which, offset).wait_send()
     for offset in range(1, tiles):
         back_out(offset).wait_send()
-    for step in range(1, WIN):
-        @pl.when((me < frames - 1) & (me >= step))
-        def _():
-            copies[step].wait_send()
-
-    @pl.when(me < frames - 1)
-    def _():
+    for step in range(WIN):
         for p in range(tiles):
-            first_hop(p).wait_send()
+            @pl.when((me < frames - 1) & (me >= step))
+            def _():
+                hop(step, p).wait_send()
 
 
 def fused_attend(frames, tiles, use, gains, bits, q, k, v):
@@ -281,10 +278,8 @@
             pltpu.SemaphoreType.DMA((4, tiles)),
             pltpu.SemaphoreType.DMA((4, tiles)),
             pltpu.SemaphoreType.DMA((4,)),
-            pltpu.SemaphoreType.DMA((WIN,)),
-            pltpu.SemaphoreType.DMA((WIN,)),
-            pltpu.SemaphoreType.DMA((tiles,)),
-            pltpu.SemaphoreType.DMA((tiles,)),
+            pltpu.SemaphoreType.DMA((WIN, tiles)),
+            pltpu.SemaphoreType.DMA((WIN, tiles)),
         ],
         compiler_params=pltpu.CompilerParams(
             collective_id=0, has_side_effects=True, vmem_limit_bytes=56 * 1024 * 1024

time: 154 us -> 165 us (1.071)
  Pallas kernels: 149 us -> 160 us
    pallas_call x1, Pallas kernels: 149 us -> 160 us  [fused_attend(): pl.pallas_call(functools.partial(fused_kernel, frames, tiles), out_shape=...]
where the time goes in v3:
time: 165 us
  Pallas kernels  160 us (97%)
  local copies, waits for them, and re-layouts  2.6 us (2%)
    pallas_call x1, Pallas kernels, fused_attend(): pl.pallas_call(functools.partial(fused_kernel, frames, tiles), out_shape=...  160 us

profile of v3, /device:TPU:224, one launch (start us, length us, event | category | flops | bytes accessed | tf_op | source)
XLA Modules:
  0.0 165.0 jit_solution(12592271297466673628)
XLA Ops:
  0.0 0.0 copy-start
  0.7 0.0 copy-start.2
  1.3 0.0 copy-start.1
  1.3 0.0 copy-done
  1.4 0.1 convolution_bitcast_fusion
  1.5 0.6 dynamic_slice.6.gain_ref
  2.1 0.0 copy-done.2
  2.1 0.6 fusion.2.use_ref
  2.7 0.0 copy-done.1
  2.7 0.1 select_reduce_fusion
  2.8 0.5 broadcast_or_fusion.bits_ref
  3.3 159.7 %shard_map.82 = bf16[64,5120]{1,0:T(8,128)(2,1)} custom-call(s32[5]{0:T(128)} %fusion.2.use_ref, f32[5]{0:T(128)} %dynamic_slice.6.gain_ref, s32[5]{0:T(128)} %broadcast_or_fusion.bits_ref, bf16[64,5120]{1,0:T(8,128)(2,1)} %bitcast.21, bf16[64,5120]{1,0:T(8,128)(2,1)} %bitcast.22, bf16[64,5120]{1,0:T(8,128)(2,1)} %bitcast.23), custom_call_target="tpu_custom_call" | custom-call | flops 4026531840 | bytes 14417920 | tf_op jit(solution)/shard_map/pallas_call | solution.py:263
  163.0 2.0 %copy.12 = bf16[1,1,64,5120]{3,2,1,0:T(8,128)(2,1)} copy(bf16[1,1,64,5120]{3,2,1,0:T(8,128)(2,1)} %bitcast.20) | data formatting | bytes 1310720
  (1 shorter events, 0.0 us)
Async XLA Ops:
  0.0 1.3 copy-start
  0.7 1.4 copy-start.2
  1.3 1.3 copy-start.1

commit v4 on v3

--- a/solution.py
+++ b/solution.py
@@ -127,15 +127,15 @@
     for which in range(2):
         locals_[which].wait()
     for offset in early:
-        p = sender_of(offset)
         if offset:
             for which in range(2):
                 piece_in(which, offset).wait_recv()
-        pass_on(0, p)
-        for step in range(1, WIN):
-            take(step - 1, p)
-            pass_on(step, p)
-        take(WIN - 1, p)
+        pass_on(0, sender_of(offset))
+    for step in range(1, WIN + 1):
+        for offset in early:
+            take(step - 1, sender_of(offset))
+            if step < WIN:
+                pass_on(step, sender_of(offset))
 
     for c in range(frame_tok // CHUNK):
         query_pos = c * CHUNK + lax.broadcasted_iota(jnp.int32, (CHUNK, frame_tok), 0)

time: 165 us -> 155 us (0.939)
  Pallas kernels: 160 us -> 149 us
    pallas_call x1, Pallas kernels: 160 us -> 149 us  [fused_attend(): pl.pallas_call(functools.partial(fused_kernel, frames, tiles), out_shape=...]
where the time goes in v4:
time: 155 us; the launch traced here: 154 us
  Pallas kernels  149 us (96%)
  local copies, waits for them, and re-layouts  2.6 us (2%)
    pallas_call x1, Pallas kernels, fused_attend(): pl.pallas_call(functools.partial(fused_kernel, frames, tiles), out_shape=...  149 us

profile of v4, /device:TPU:224, one launch (start us, length us, event | category | flops | bytes accessed | tf_op | source)
XLA Modules:
  0.0 154.4 jit_solution(8253096814495375447)
XLA Ops:
  0.0 0.0 copy-start
  0.7 0.0 copy-start.2
  1.3 0.0 copy-start.1
  1.3 0.0 copy-done
  1.4 0.1 convolution_bitcast_fusion
  1.5 0.6 dynamic_slice.6.gain_ref
  2.1 0.0 copy-done.2
  2.1 0.6 fusion.2.use_ref
  2.7 0.0 copy-done.1
  2.7 0.1 select_reduce_fusion
  2.8 0.5 broadcast_or_fusion.bits_ref
  3.3 149.1 %shard_map.82 = bf16[64,5120]{1,0:T(8,128)(2,1)} custom-call(s32[5]{0:T(128)} %fusion.2.use_ref, f32[5]{0:T(128)} %dynamic_slice.6.gain_ref, s32[5]{0:T(128)} %broadcast_or_fusion.bits_ref, bf16[64,5120]{1,0:T(8,128)(2,1)} %bitcast.21, bf16[64,5120]{1,0:T(8,128)(2,1)} %bitcast.22, bf16[64,5120]{1,0:T(8,128)(2,1)} %bitcast.23), custom_call_target="tpu_custom_call" | custom-call | flops 4026531840 | bytes 14417920 | tf_op jit(solution)/shard_map/pallas_call | solution.py:263
  152.4 2.0 %copy.12 = bf16[1,1,64,5120]{3,2,1,0:T(8,128)(2,1)} copy(bf16[1,1,64,5120]{3,2,1,0:T(8,128)(2,1)} %bitcast.20) | data formatting | bytes 1310720
  (1 shorter events, 0.0 us)
Async XLA Ops:
  0.0 1.3 copy-start
  0.7 1.4 copy-start.2
  1.3 1.3 copy-start.1

commit v5 on v2

--- a/solution.py
+++ b/solution.py
@@ -15,7 +15,7 @@
 BLK = 4
 WIN = 5
 STEPS = 4
-CHUNK = 256
+CHUNK = 128
 
 NEG_BIG = -1e30
 MESH_ID = pl.DeviceIdType.MESH
@@ -168,13 +168,12 @@
                 if use is None:
                     code = code_scr[rows, :]
                     shifted = lax.shift_right_logical(jnp.broadcast_to(bits_ref[h], code.shape), code)
-                    allowed = (shifted & 1) == 1
+                    scores = jnp.where((shifted & 1) == 1, scores, NEG_BIG)
                 else:
-                    allowed = jnp.broadcast_to(use > 0, scores.shape)
-                scores = jnp.where(allowed, scores, NEG_BIG)
+                    scores = scores + jnp.where(use > 0, 0.0, NEG_BIG)
                 old_max = m_scr[h, rows, :]
                 new_max = jnp.maximum(old_max, jnp.max(scores, axis=1, keepdims=True))
-                weights = jnp.where(allowed, jnp.exp(scores - new_max), 0.0)
+                weights = jnp.exp(scores - new_max)
                 factor = jnp.exp(old_max - new_max)
                 l_scr[h, rows, :] = l_scr[h, rows, :] * factor + jnp.sum(weights, axis=1, keepdims=True)
                 acc_scr[h, rows, :] = acc_scr[h, rows, :] * factor + jnp.dot(

time: 154 us -> 154 us (level)
  no operation moved by 1% of the time
where the time goes in v5:
time: 154 us; the launch traced here: 153 us
  Pallas kernels  148 us (96%)
  local copies, waits for them, and re-layouts  2.6 us (2%)
    pallas_call x1, Pallas kernels, fused_attend(): pl.pallas_call(functools.partial(fused_kernel, frames, tiles), out_shape=...  148 us

profile of v5, /device:TPU:224, one launch (start us, length us, event | category | flops | bytes accessed | tf_op | source)
XLA Modules:
  0.0 153.4 jit_solution(7903661655507188802)
XLA Ops:
  0.0 0.0 copy-start
  0.7 0.0 copy-start.2
  1.3 0.0 copy-start.1
  1.3 0.0 copy-done
  1.4 0.1 convolution_bitcast_fusion
  1.5 0.6 dynamic_slice.6.gain_ref
  2.1 0.0 copy-done.2
  2.1 0.6 fusion.2.use_ref
  2.7 0.0 copy-done.1
  2.7 0.1 select_reduce_fusion
  2.8 0.5 broadcast_or_fusion.bits_ref
  3.3 148.2 %shard_map.82 = bf16[64,5120]{1,0:T(8,128)(2,1)} custom-call(s32[5]{0:T(128)} %fusion.2.use_ref, f32[5]{0:T(128)} %dynamic_slice.6.gain_ref, s32[5]{0:T(128)} %broadcast_or_fusion.bits_ref, bf16[64,5120]{1,0:T(8,128)(2,1)} %bitcast.21, bf16[64,5120]{1,0:T(8,128)(2,1)} %bitcast.22, bf16[64,5120]{1,0:T(8,128)(2,1)} %bitcast.23), custom_call_target="tpu_custom_call" | custom-call | flops 4026531840 | bytes 14417920 | tf_op jit(solution)/shard_map/pallas_call | solution.py:265
  151.4 2.0 %copy.12 = bf16[1,1,64,5120]{3,2,1,0:T(8,128)(2,1)} copy(bf16[1,1,64,5120]{3,2,1,0:T(8,128)(2,1)} %bitcast.20) | data formatting | bytes 1310720
  (1 shorter events, 0.0 us)
Async XLA Ops:
  0.0 1.3 copy-start
  0.7 1.4 copy-start.2
  1.3 1.3 copy-start.1

commit v6 on v5

--- a/solution.py
+++ b/solution.py
@@ -32,7 +32,8 @@
 
 def fused_kernel(frames, tiles, use_ref, gain_ref, bits_ref, q_ref, k_ref, v_ref, out_ref,
                  own_kv, own_q, slots, fin, got_out, code_scr, m_scr, l_scr, acc_scr,
-                 piece_send, piece_recv, local_sem, send_sem, recv_sem, hop_send, hop_recv):
+                 piece_send, piece_recv, local_sem, send_sem, recv_sem, hop_send, hop_recv,
+                 out_send, out_recv, home_sem):
     me = lax.axis_index("frame")
     tile = lax.axis_index("tile")
     right = lax.rem(me + 1, frames)
@@ -153,8 +154,8 @@
     for offset in range(1, tiles):
         piece_in(2, offset).wait_recv()
 
-    def attend(block, use):
-        def head_body(h, carry):
+    def attend_head(block, use, h):
+        if True:
             col = pl.multiple_of(h * HD, HD)
             key_h = block[0, :, pl.ds(col, HD)]
             value_h = block[1, :, pl.ds(col, HD)]
@@ -180,6 +181,10 @@
                     weights.astype(jnp.bfloat16), value_h, preferred_element_type=jnp.float32
                 )
                 m_scr[h, rows, :] = new_max
+
+    def attend(block, use):
+        def head_body(h, carry):
+            attend_head(block, use, h)
             return carry
 
         lax.fori_loop(0, head_share, head_body, 0)
@@ -197,52 +202,61 @@
                 @pl.when(me < frames - 1)
                 def _():
                     copies[step].start()
-            attend(slots.at[step - 1], use_ref[step - 1])
-
-    def finish(h, carry):
-        col = pl.multiple_of(h * HD, HD)
-        fin[:, pl.ds(col, HD)] = (acc_scr[h] / l_scr[h] * gain_ref[h]).astype(fin.dtype)
-        return carry
-
-    lax.fori_loop(0, head_share, finish, 0)
-
-    def back_out(offset):
+                attend(slots.at[step - 1], use_ref[step - 1])
+
+    def head_cols(p, h):
+        return pl.ds(pl.multiple_of(p * share + h * HD, HD), HD)
+
+    def back_out(offset, h):
         peer = lax.rem(tile + offset, tiles)
         return pltpu.make_async_remote_copy(
-            src_ref=fin.at[tokens_of(peer), :],
-            dst_ref=got_out.at[:, channels_of(tile)],
-            send_sem=piece_send.at[3, offset],
-            recv_sem=piece_recv.at[3, tile],
+            src_ref=fin.at[tokens_of(peer), pl.ds(h * HD, HD)],
+            dst_ref=got_out.at[:, head_cols(tile, h)],
+            send_sem=out_send.at[offset, h],
+            recv_sem=out_recv.at[tile, h],
             device_id=(me, peer),
             device_id_type=MESH_ID,
         )
 
-    def back_in(offset):
+    def back_in(offset, h):
         sender = lax.rem(tile + tiles - offset, tiles)
         return pltpu.make_async_remote_copy(
-            src_ref=fin.at[tokens_of(tile), :],
-            dst_ref=got_out.at[:, channels_of(sender)],
-            send_sem=piece_send.at[3, offset],
-            recv_sem=piece_recv.at[3, sender],
+            src_ref=fin.at[tokens_of(tile), pl.ds(h * HD, HD)],
+            dst_ref=got_out.at[:, head_cols(sender, h)],
+            send_sem=out_send.at[offset, h],
+            recv_sem=out_recv.at[sender, h],
             device_id=(me, sender),
             device_id_type=MESH_ID,
         )
 
-    home = pltpu.make_async_copy(fin.at[tokens_of(tile), :], got_out.at[:, channels_of(tile)],
-                                 local_sem.at[3])
-    home.start()
-    for offset in range(1, tiles):
-        back_out(offset).start()
-    home.wait()
-    for offset in range(1, tiles):
-        back_in(offset).wait_recv()
+    def home(h):
+        return pltpu.make_async_copy(
+            fin.at[tokens_of(tile), pl.ds(h * HD, HD)], got_out.at[:, head_cols(tile, h)],
+            home_sem.at[h],
+        )
+
+    for h in range(head_share):
+        @pl.when(me >= WIN)
+        def _():
+            attend_head(slots.at[WIN - 1], use_ref[WIN - 1], h)
+
+        fin[:, pl.ds(h * HD, HD)] = (acc_scr[h] / l_scr[h] * gain_ref[h]).astype(fin.dtype)
+        home(h).start()
+        for offset in far_first:
+            back_out(offset, h).start()
+
+    for h in range(head_share):
+        home(h).wait()
+        for offset in near_first:
+            back_in(offset, h).wait_recv()
     out_ref[...] = got_out[...]
 
     for which in range(3):
         for offset in range(1, tiles):
             piece_out(which, offset).wait_send()
-    for offset in range(1, tiles):
-        back_out(offset).wait_send()
+    for h in range(head_share):
+        for offset in range(1, tiles):
+            back_out(offset, h).wait_send()
     for step in range(1, WIN):
         @pl.when((me < frames - 1) & (me >= step))
         def _():
@@ -284,6 +298,9 @@
             pltpu.SemaphoreType.DMA((WIN,)),
             pltpu.SemaphoreType.DMA((tiles,)),
             pltpu.SemaphoreType.DMA((tiles,)),
+            pltpu.SemaphoreType.DMA((tiles, head_share)),
+            pltpu.SemaphoreType.DMA((tiles, head_share)),
+            pltpu.SemaphoreType.DMA((head_share,)),
         ],
         compiler_params=pltpu.CompilerParams(
             collective_id=0, has_side_effects=True, vmem_limit_bytes=56 * 1024 * 1024

time: 154 us -> 154 us (level)
  no operation moved by 1% of the time
where the time goes in v6:
time: 154 us
  Pallas kernels  149 us (97%)
  local copies, waits for them, and re-layouts  2.6 us (2%)
    pallas_call x1, Pallas kernels, fused_attend(): pl.pallas_call(functools.partial(fused_kernel, frames, tiles), out_shape=...  149 us

profile of v6, /device:TPU:224, one launch (start us, length us, event | category | flops | bytes accessed | tf_op | source)
XLA Modules:
  0.0 154.0 jit_solution(5875445673239243432)
XLA Ops:
  0.0 0.0 copy-start
  0.7 0.0 copy-start.2
  1.3 0.0 copy-start.1
  1.3 0.0 copy-done
  1.4 0.1 convolution_bitcast_fusion
  1.5 0.6 dynamic_slice.6.gain_ref
  2.1 0.0 copy-done.2
  2.1 0.6 fusion.2.use_ref
  2.7 0.0 copy-done.1
  2.7 0.1 select_reduce_fusion
  2.8 0.5 broadcast_or_fusion.bits_ref
  3.3 148.7 %shard_map.82 = bf16[64,5120]{1,0:T(8,128)(2,1)} custom-call(s32[5]{0:T(128)} %fusion.2.use_ref, f32[5]{0:T(128)} %dynamic_slice.6.gain_ref, s32[5]{0:T(128)} %broadcast_or_fusion.bits_ref, bf16[64,5120]{1,0:T(8,128)(2,1)} %bitcast.21, bf16[64,5120]{1,0:T(8,128)(2,1)} %bitcast.22, bf16[64,5120]{1,0:T(8,128)(2,1)} %bitcast.23), custom_call_target="tpu_custom_call" | custom-call | flops 4026531840 | bytes 14417920 | tf_op jit(solution)/shard_map/pallas_call | solution.py:279
  152.0 2.0 %copy.12 = bf16[1,1,64,5120]{3,2,1,0:T(8,128)(2,1)} copy(bf16[1,1,64,5120]{3,2,1,0:T(8,128)(2,1)} %bitcast.20) | data formatting | bytes 1310720
  (1 shorter events, 0.0 us)
Async XLA Ops:
  0.0 1.3 copy-start
  0.7 1.4 copy-start.2
  1.3 1.3 copy-start.1

commit v7 on v5

--- a/solution.py
+++ b/solution.py
@@ -30,7 +30,7 @@
     return row // BLK, col // BLK
 
 
-def fused_kernel(frames, tiles, use_ref, gain_ref, bits_ref, q_ref, k_ref, v_ref, out_ref,
+def fused_kernel(frames, tiles, step_ref, fidx_ref, wm_ref, hm_ref, sg_ref, q_ref, k_ref, v_ref, out_ref,
                  own_kv, own_q, slots, fin, got_out, code_scr, m_scr, l_scr, acc_scr,
                  piece_send, piece_recv, local_sem, send_sem, recv_sem, hop_send, hop_recv):
     me = lax.axis_index("frame")
@@ -42,6 +42,19 @@
     share = own_q.shape[1]
     tile_tok = q_ref.shape[0]
     scale = 1.0 / math.sqrt(HD)
+
+    def head_bits(h):
+        row = tile * head_share + h
+        bits = 16
+        for offset in range(9):
+            bits = bits | jnp.where(wm_ref[row, offset] == 1, 1 << offset, 0)
+        return bits
+
+    def usable(distance):
+        return (hm_ref[0, distance - 1] == 1) & (distance <= fidx_ref[0]) & (me >= distance)
+
+    def head_gain(h):
+        return sg_ref[step_ref[0], tile * head_share + h]
 
     barrier = pltpu.get_barrier_semaphore()
     for other in (left, right):
@@ -167,10 +180,10 @@
                 ) * scale
                 if use is None:
                     code = code_scr[rows, :]
-                    shifted = lax.shift_right_logical(jnp.broadcast_to(bits_ref[h], code.shape), code)
+                    shifted = lax.shift_right_logical(jnp.broadcast_to(head_bits(h), code.shape), code)
                     scores = jnp.where((shifted & 1) == 1, scores, NEG_BIG)
                 else:
-                    scores = scores + jnp.where(use > 0, 0.0, NEG_BIG)
+                    scores = scores + jnp.where(use, 0.0, NEG_BIG)
                 old_max = m_scr[h, rows, :]
                 new_max = jnp.maximum(old_max, jnp.max(scores, axis=1, keepdims=True))
                 weights = jnp.exp(scores - new_max)
@@ -197,11 +210,11 @@
                 @pl.when(me < frames - 1)
                 def _():
                     copies[step].start()
-            attend(slots.at[step - 1], use_ref[step - 1])
+            attend(slots.at[step - 1], usable(step))
 
     def finish(h, carry):
         col = pl.multiple_of(h * HD, HD)
-        fin[:, pl.ds(col, HD)] = (acc_scr[h] / l_scr[h] * gain_ref[h]).astype(fin.dtype)
+        fin[:, pl.ds(col, HD)] = (acc_scr[h] / l_scr[h] * head_gain(h)).astype(fin.dtype)
         return carry
 
     lax.fori_loop(0, head_share, finish, 0)
@@ -254,18 +267,19 @@
             first_hop(p).wait_send()
 
 
-def fused_attend(frames, tiles, use, gains, bits, q, k, v):
-    head_share = gains.shape[0]
+def fused_attend(frames, tiles, scalars, q, k, v):
+    head_share = HEADS // tiles
     tile_tok, channels = q.shape
     frame_tok = tile_tok * tiles
     share = channels // tiles
     flops = 4 * (WIN + 1) * frame_tok * frame_tok * share
     smem = pl.BlockSpec(memory_space=pltpu.SMEM)
     vmem = pl.BlockSpec(memory_space=pltpu.VMEM)
+    hbm = pl.BlockSpec(memory_space=pl.ANY)
     return pl.pallas_call(
         functools.partial(fused_kernel, frames, tiles),
         out_shape=jax.ShapeDtypeStruct(q.shape, jnp.bfloat16),
-        in_specs=[smem, smem, smem, vmem, vmem, vmem],
+        in_specs=[smem] * len(scalars) + [hbm] * 3,
         out_specs=vmem,
         scratch_shapes=[
             pltpu.VMEM((2, frame_tok, share), jnp.bfloat16),
@@ -293,7 +307,7 @@
             transcendentals=(WIN + 1) * head_share * frame_tok * frame_tok,
             bytes_accessed=(WIN + 6) * 2 * frame_tok * share * 2,
         ),
-    )(use, gains, bits, q, k, v)
+    )(*scalars, q, k, v)
 
 
 def shards(queries, keys, values, step_index, frame_index, window_mask, history_mask, step_gain):
@@ -305,19 +319,8 @@
     head_share = HEADS // tile_count
     tile_tok = queries.shape[2]
     frame_tok = tile_tok * tile_count
-    picker = (jnp.arange(STEPS, dtype=jnp.int32) == step_index[0]).astype(jnp.float32)
-    head_gains = jnp.dot(picker, step_gain, precision=lax.Precision.HIGHEST)
-    my_gains = lax.dynamic_slice_in_dim(head_gains, tile_id * head_share, head_share)
-    my_masks = lax.dynamic_slice_in_dim(window_mask, tile_id * head_share, head_share, axis=0)
-    distance = jnp.arange(1, WIN + 1, dtype=jnp.int32)
-    use = (
-        (history_mask[0] == 1) & (distance <= frame_index[0]) & (group_id - distance >= 0)
-    ).astype(jnp.int32)
-    bits = jnp.sum(
-        jnp.where(my_masks == 1, jnp.left_shift(1, jnp.arange(9, dtype=jnp.int32)), 0), axis=1
-    ) | 16
     finished = fused_attend(
-        frames, tile_count, use, my_gains, bits.astype(jnp.int32),
+        frames, tile_count, (step_index, frame_index, window_mask, history_mask, step_gain),
         queries[0, 0], keys[0, 0], values[0, 0],
     )
     return finished.reshape(1, 1, tile_tok, channels)

time: 154 us -> 153 us (level)
  no operation moved by 1% of the time
where the time goes in v7:
time: 153 us; the launch traced here: 152 us
  Pallas kernels  148 us (97%)
  local copies, waits for them, and re-layouts  2.66 us (2%)
    pallas_call x1, Pallas kernels, fused_attend(): pl.pallas_call(functools.partial(fused_kernel, frames, tiles), out_shape=...  148 us

profile of v7, /device:TPU:224, one launch (start us, length us, event | category | flops | bytes accessed | tf_op | source)
XLA Modules:
  0.0 151.9 jit_solution(6263358956917961096)
XLA Ops:
  0.0 0.0 copy-start
  1.3 0.0 copy-done
  1.3 0.7 copy.9.wm_ref
  2.0 147.9 %shard_map.82 = bf16[64,5120]{1,0:T(8,128)(2,1)} custom-call(s32[1]{0:T(128)S(6)} %copy.11.step_ref, s32[1]{0:T(128)S(6)} %copy.12.fidx_ref, s32[40,9]{1,0:T(8,128)} %copy.9.wm_ref, s32[1,5]{1,0:T(1,128)} %hm_ref.1, f32[4,40]{1,0:T(4,128)} %sg_ref.1, bf16[64,5120]{1,0:T(8,128)(2,1)} %bitcast.5, bf16[64,5120]{1,0:T(8,128)(2,1)} %bitcast.6, ...), custom_call_target="tpu_custom_call" | custom-call | flops 4026531840 | bytes 14417920 | tf_op jit(solution)/shard_map/pallas_call | solution.py:279
  149.9 2.0 %copy.13 = bf16[1,1,64,5120]{3,2,1,0:T(8,128)(2,1)} copy(bf16[1,1,64,5120]{3,2,1,0:T(8,128)(2,1)} %bitcast.4) | data formatting | bytes 1310720
Async XLA Ops:
  0.0 1.3 copy-start

commit v8 on v7

--- a/solution.py
+++ b/solution.py
@@ -16,6 +16,7 @@
 WIN = 5
 STEPS = 4
 CHUNK = 128
+GROUP = 8
 
 NEG_BIG = -1e30
 MESH_ID = pl.DeviceIdType.MESH
@@ -32,7 +33,8 @@
 
 def fused_kernel(frames, tiles, step_ref, fidx_ref, wm_ref, hm_ref, sg_ref, q_ref, k_ref, v_ref, out_ref,
                  own_kv, own_q, slots, fin, got_out, code_scr, m_scr, l_scr, acc_scr,
-                 piece_send, piece_recv, local_sem, send_sem, recv_sem, hop_send, hop_recv):
+                 piece_send, piece_recv, local_sem, send_sem, recv_sem, hop_send, hop_recv,
+                 direct_send, direct_recv):
     me = lax.axis_index("frame")
     tile = lax.axis_index("tile")
     right = lax.rem(me + 1, frames)
@@ -57,12 +59,13 @@
         return sg_ref[step_ref[0], tile * head_share + h]
 
     barrier = pltpu.get_barrier_semaphore()
-    for other in (left, right):
-        pl.semaphore_signal(barrier, inc=1, device_id=(other, tile), device_id_type=MESH_ID)
+    for distance in range(1, WIN + 1):
+        for other in (lax.rem(me + frames - distance, frames), lax.rem(me + distance, frames)):
+            pl.semaphore_signal(barrier, inc=1, device_id=(other, tile), device_id_type=MESH_ID)
     for offset in range(1, tiles):
         peer = lax.rem(tile + offset, tiles)
         pl.semaphore_signal(barrier, inc=1, device_id=(me, peer), device_id_type=MESH_ID)
-    pl.semaphore_wait(barrier, 2 + tiles - 1)
+    pl.semaphore_wait(barrier, 2 * WIN + tiles - 1)
 
     def channels_of(p):
         return pl.ds(pl.multiple_of(p * share, 128), share)
@@ -157,6 +160,28 @@
         )
 
     copies = [None] + [copy_for(step) for step in range(1, WIN)]
+
+    position = lax.rem(me, GROUP)
+    group_start = (position == 0) & (me >= GROUP)
+    before_start = position == GROUP - 1
+
+    def direct(distance):
+        return pltpu.make_async_remote_copy(
+            src_ref=own_kv,
+            dst_ref=slots.at[distance - 1],
+            send_sem=direct_send.at[distance - 1],
+            recv_sem=direct_recv.at[distance - 1],
+            device_id=(lax.rem(me + distance, frames), tile),
+            device_id_type=MESH_ID,
+        )
+
+    def direct_sender(distance):
+        return (position == GROUP - distance) & (me + distance < frames)
+
+    for distance in range(2, WIN + 1):
+        @pl.when(direct_sender(distance))
+        def _():
+            direct(distance).start()
 
     m_scr[...] = jnp.full(m_scr.shape, NEG_BIG, jnp.float32)
     l_scr[...] = jnp.zeros(l_scr.shape, jnp.float32)
@@ -205,9 +230,15 @@
                 for p in range(tiles):
                     first_hop(p).wait_recv()
             else:
-                copies[step - 1].wait_recv()
+                @pl.when(group_start)
+                def _():
+                    direct(step).wait_recv()
+
+                @pl.when(jnp.logical_not(group_start))
+                def _():
+                    copies[step - 1].wait_recv()
             if step < WIN:
-                @pl.when(me < frames - 1)
+                @pl.when((me < frames - 1) & jnp.logical_not(before_start))
                 def _():
                     copies[step].start()
             attend(slots.at[step - 1], usable(step))
@@ -257,9 +288,14 @@
     for offset in range(1, tiles):
         back_out(offset).wait_send()
     for step in range(1, WIN):
-        @pl.when((me < frames - 1) & (me >= step))
+        @pl.when((me < frames - 1) & (me >= step) & jnp.logical_not(before_start))
         def _():
             copies[step].wait_send()
+
+    for distance in range(2, WIN + 1):
+        @pl.when(direct_sender(distance))
+        def _():
+            direct(distance).wait_send()
 
     @pl.when(me < frames - 1)
     def _():
@@ -298,6 +334,8 @@
             pltpu.SemaphoreType.DMA((WIN,)),
             pltpu.SemaphoreType.DMA((tiles,)),
             pltpu.SemaphoreType.DMA((tiles,)),
+            pltpu.SemaphoreType.DMA((WIN,)),
+            pltpu.SemaphoreType.DMA((WIN,)),
         ],
         compiler_params=pltpu.CompilerParams(
             collective_id=0, has_side_effects=True, vmem_limit_bytes=56 * 1024 * 1024

time: 153 us -> 180 us (1.18)
  the two profiles are of different devices: /device:TPU:224 before, /device:TPU:162 now
where the time goes in v8:
time: 180 us
  Pallas kernels  176 us (98%)
  local copies, waits for them, and re-layouts  2.66 us (1%)
    pallas_call x1, Pallas kernels, fused_attend(): pl.pallas_call(functools.partial(fused_kernel, frames, tiles), out_shape=...  176 us

profile of v8, /device:TPU:162, one launch (start us, length us, event | category | flops | bytes accessed | tf_op | source)
XLA Modules:
  0.0 180.0 jit_solution(3164901910836264631)
XLA Ops:
  0.0 0.0 copy-start
  1.3 0.0 copy-done
  1.3 0.7 copy.9.wm_ref
  2.0 176.0 %shard_map.82 = bf16[64,5120]{1,0:T(8,128)(2,1)} custom-call(s32[1]{0:T(128)S(6)} %copy.11.step_ref, s32[1]{0:T(128)S(6)} %copy.12.fidx_ref, s32[40,9]{1,0:T(8,128)} %copy.9.wm_ref, s32[1,5]{1,0:T(1,128)} %hm_ref.1, f32[4,40]{1,0:T(4,128)} %sg_ref.1, bf16[64,5120]{1,0:T(8,128)(2,1)} %bitcast.5, bf16[64,5120]{1,0:T(8,128)(2,1)} %bitcast.6, ...), custom_call_target="tpu_custom_call" | custom-call | flops 4026531840 | bytes 14417920 | tf_op jit(solution)/shard_map/pallas_call | solution.py:315
  178.0 2.0 %copy.13 = bf16[1,1,64,5120]{3,2,1,0:T(8,128)(2,1)} copy(bf16[1,1,64,5120]{3,2,1,0:T(8,128)(2,1)} %bitcast.4) | data formatting | bytes 1310720
Async XLA Ops:
  0.0 1.3 copy-start

commit v9 on v7

--- a/solution.py
+++ b/solution.py
@@ -310,6 +310,21 @@
     )(*scalars, q, k, v)
 
 
+def hand_over_kernel(src_ref, dst_ref):
+    dst_ref[...] = src_ref[...]
+
+
+def hand_over(block):
+    vmem = pl.BlockSpec(memory_space=pltpu.VMEM)
+    return pl.pallas_call(
+        hand_over_kernel,
+        out_shape=jax.ShapeDtypeStruct(block.shape, block.dtype),
+        in_specs=[vmem],
+        out_specs=vmem,
+        cost_estimate=pl.CostEstimate(flops=0, transcendentals=0, bytes_accessed=2 * block.size * 2),
+    )(block)
+
+
 def shards(queries, keys, values, step_index, frame_index, window_mask, history_mask, step_gain):
     tile_count = lax.axis_size("tile")
     frames = lax.axis_size("frame")
@@ -323,7 +338,7 @@
         frames, tile_count, (step_index, frame_index, window_mask, history_mask, step_gain),
         queries[0, 0], keys[0, 0], values[0, 0],
     )
-    return finished.reshape(1, 1, tile_tok, channels)
+    return hand_over(finished).reshape(1, 1, tile_tok, channels)
 
 
 def solution(mesh):

time: 153 us -> 153 us (level)
  Pallas kernels: 148 us -> 150 us
  local copies, waits for them, and re-layouts: 2.66 us -> 0.7 us
    pallas_call x0 -> x1, Pallas kernels: none -> 1.97 us  [hand_over(): pl.pallas_call(hand_over_kernel, out_shape=jax.ShapeDtypeStruct(block.sha...]
    unnamed x4 -> x3, local copies, waits for them, and re-layouts: 2.66 us -> 0.7 us
where the time goes in v9:
time: 153 us; the launch traced here: 152 us
  Pallas kernels  150 us (98%)
    pallas_call x1, Pallas kernels, fused_attend(): pl.pallas_call(functools.partial(fused_kernel, frames, tiles), out_shape=...  148 us

profile of v9, /device:TPU:224, one launch (start us, length us, event | category | flops | bytes accessed | tf_op | source)
XLA Modules:
  0.0 151.9 jit_solution(6787311964759737211)
XLA Ops:
  0.0 0.0 copy-start
  1.3 0.0 copy-done
  1.3 0.7 copy.9.wm_ref
  2.0 147.9 %shard_map.82.src_ref = bf16[64,5120]{1,0:T(8,128)(2,1)} custom-call(s32[1]{0:T(128)S(6)} %copy.10.step_ref, s32[1]{0:T(128)S(6)} %copy.11.fidx_ref, s32[40,9]{1,0:T(8,128)} %copy.9.wm_ref, s32[1,5]{1,0:T(1,128)} %hm_ref.1, f32[4,40]{1,0:T(4,128)} %sg_ref.1, bf16[64,5120]{1,0:T(8,128)(2,1)} %bitcast.4, bf16[64,5120]{1,0:T(8,128)(2,1)} %bitcast.5, ...), custom_call_target="tpu_custom_call" | custom-call | flops 4026531840 | bytes 14417920 | tf_op jit(solution)/shard_map/pallas_call | solution.py:279
  149.9 2.0 %shard_map.83 = bf16[64,5120]{1,0:T(8,128)(2,1)} custom-call(bf16[64,5120]{1,0:T(8,128)(2,1)} %shard_map.82.src_ref), custom_call_target="tpu_custom_call" | custom-call | bytes 1310720 | tf_op jit(solution)/shard_map/pallas_call | solution.py:319
Async XLA Ops:
  0.0 1.3 copy-start

commit v10 on v9

--- a/solution.py
+++ b/solution.py
@@ -47,7 +47,7 @@
         row = tile * head_share + h
         bits = 16
         for offset in range(9):
-            bits = bits | jnp.where(wm_ref[row, offset] == 1, 1 << offset, 0)
+            bits = bits | jnp.where(wm_ref[offset, row] == 1, 1 << offset, 0)
         return bits
 
     def usable(distance):
@@ -335,7 +335,7 @@
     tile_tok = queries.shape[2]
     frame_tok = tile_tok * tile_count
     finished = fused_attend(
-        frames, tile_count, (step_index, frame_index, window_mask, history_mask, step_gain),
+        frames, tile_count, (step_index, frame_index, window_mask.T, history_mask, step_gain),
         queries[0, 0], keys[0, 0], values[0, 0],
     )
     return hand_over(finished).reshape(1, 1, tile_tok, channels)

time: 153 us -> 152 us (level)
  no operation moved by 1% of the time
where the time goes in v10:
time: 152 us; the launch traced here: 151 us
  Pallas kernels  150 us (99%)
    pallas_call x1, Pallas kernels, fused_attend(): pl.pallas_call(functools.partial(fused_kernel, frames, tiles), out_shape=...  148 us

profile of v10, /device:TPU:224, one launch (start us, length us, event | category | flops | bytes accessed | tf_op | source)
XLA Modules:
  0.0 151.1 jit_solution(12482732576870068762)
XLA Ops:
  1.3 147.8 %shard_map.82.src_ref = bf16[64,5120]{1,0:T(8,128)(2,1)} custom-call(s32[1]{0:T(128)S(6)} %copy.9.step_ref, s32[1]{0:T(128)S(6)} %copy.10.fidx_ref, s32[9,40]{1,0:T(8,128)} %bitcast.8, s32[1,5]{1,0:T(1,128)} %hm_ref.1, f32[4,40]{1,0:T(4,128)} %sg_ref.1, bf16[64,5120]{1,0:T(8,128)(2,1)} %bitcast.5, bf16[64,5120]{1,0:T(8,128)(2,1)} %bitcast.6, ...), custom_call_target="tpu_custom_call" | custom-call | flops 4026531840 | bytes 14417920 | tf_op jit(solution)/shard_map/pallas_call | solution.py:279
  149.1 2.0 %shard_map.83 = bf16[64,5120]{1,0:T(8,128)(2,1)} custom-call(bf16[64,5120]{1,0:T(8,128)(2,1)} %shard_map.82.src_ref), custom_call_target="tpu_custom_call" | custom-call | bytes 1310720 | tf_op jit(solution)/shard_map/pallas_call | solution.py:319

commit v11 on v10

--- a/solution.py
+++ b/solution.py
@@ -244,10 +244,10 @@
     home = pltpu.make_async_copy(fin.at[tokens_of(tile), :], got_out.at[:, channels_of(tile)],
                                  local_sem.at[3])
     home.start()
-    for offset in range(1, tiles):
+    for offset in far_first:
         back_out(offset).start()
     home.wait()
-    for offset in range(1, tiles):
+    for offset in near_first:
         back_in(offset).wait_recv()
     out_ref[...] = got_out[...]
 

time: 152 us -> 152 us (level)
  no operation moved by 1% of the time
where the time goes in v11:
time: 152 us; the launch traced here: 151 us
  Pallas kernels  150 us (99%)
    pallas_call x1, Pallas kernels, fused_attend(): pl.pallas_call(functools.partial(fused_kernel, frames, tiles), out_shape=...  148 us

profile of v11, /device:TPU:224, one launch (start us, length us, event | category | flops | bytes accessed | tf_op | source)
XLA Modules:
  0.0 151.1 jit_solution(8022250395127724629)
XLA Ops:
  1.3 147.8 %shard_map.82.src_ref = bf16[64,5120]{1,0:T(8,128)(2,1)} custom-call(s32[1]{0:T(128)S(6)} %copy.9.step_ref, s32[1]{0:T(128)S(6)} %copy.10.fidx_ref, s32[9,40]{1,0:T(8,128)} %bitcast.8, s32[1,5]{1,0:T(1,128)} %hm_ref.1, f32[4,40]{1,0:T(4,128)} %sg_ref.1, bf16[64,5120]{1,0:T(8,128)(2,1)} %bitcast.5, bf16[64,5120]{1,0:T(8,128)(2,1)} %bitcast.6, ...), custom_call_target="tpu_custom_call" | custom-call | flops 4026531840 | bytes 14417920 | tf_op jit(solution)/shard_map/pallas_call | solution.py:279
  149.1 2.0 %shard_map.83 = bf16[64,5120]{1,0:T(8,128)(2,1)} custom-call(bf16[64,5120]{1,0:T(8,128)(2,1)} %shard_map.82.src_ref), custom_call_target="tpu_custom_call" | custom-call | bytes 1310720 | tf_op jit(solution)/shard_map/pallas_call | solution.py:319

commit v12 on v10

--- a/solution.py
+++ b/solution.py
@@ -107,8 +107,12 @@
     near_first = far_first[::-1]
     for which in range(3):
         locals_[which].start()
-        for offset in far_first:
-            piece_out(which, offset).start()
+    for group in ([j for j in far_first if j % 2], [j for j in far_first if j % 2 == 0]):
+        for which in range(2):
+            for offset in group:
+                piece_out(which, offset).start()
+    for offset in far_first:
+        piece_out(2, offset).start()
 
     for c in range(frame_tok // CHUNK):
         query_pos = c * CHUNK + lax.broadcasted_iota(jnp.int32, (CHUNK, frame_tok), 0)

time: 152 us -> 152 us (level)
  no operation moved by 1% of the time
where the time goes in v12:
time: 152 us; the launch traced here: 151 us
  Pallas kernels  150 us (99%)
    pallas_call x1, Pallas kernels, fused_attend(): pl.pallas_call(functools.partial(fused_kernel, frames, tiles), out_shape=...  148 us

profile of v12, /device:TPU:224, one launch (start us, length us, event | category | flops | bytes accessed | tf_op | source)
XLA Modules:
  0.0 151.1 jit_solution(14475109672703499738)
XLA Ops:
  1.3 147.8 %shard_map.82.src_ref = bf16[64,5120]{1,0:T(8,128)(2,1)} custom-call(s32[1]{0:T(128)S(6)} %copy.9.step_ref, s32[1]{0:T(128)S(6)} %copy.10.fidx_ref, s32[9,40]{1,0:T(8,128)} %bitcast.8, s32[1,5]{1,0:T(1,128)} %hm_ref.1, f32[4,40]{1,0:T(4,128)} %sg_ref.1, bf16[64,5120]{1,0:T(8,128)(2,1)} %bitcast.5, bf16[64,5120]{1,0:T(8,128)(2,1)} %bitcast.6, ...), custom_call_target="tpu_custom_call" | custom-call | flops 4026531840 | bytes 14417920 | tf_op jit(solution)/shard_map/pallas_call | solution.py:283
  149.1 2.0 %shard_map.83 = bf16[64,5120]{1,0:T(8,128)(2,1)} custom-call(bf16[64,5120]{1,0:T(8,128)(2,1)} %shard_map.82.src_ref), custom_call_target="tpu_custom_call" | custom-call | bytes 1310720 | tf_op jit(solution)/shard_map/pallas_call | solution.py:323

commit v13 on v10

--- a/solution.py
+++ b/solution.py
@@ -310,17 +310,20 @@
     )(*scalars, q, k, v)
 
 
-def hand_over_kernel(src_ref, dst_ref):
-    dst_ref[...] = src_ref[...]
+def hand_over_kernel(src_ref, dst_ref, sem):
+    move = pltpu.make_async_copy(src_ref, dst_ref, sem)
+    move.start()
+    move.wait()
 
 
 def hand_over(block):
-    vmem = pl.BlockSpec(memory_space=pltpu.VMEM)
+    anywhere = pl.BlockSpec(memory_space=pl.ANY)
     return pl.pallas_call(
         hand_over_kernel,
         out_shape=jax.ShapeDtypeStruct(block.shape, block.dtype),
-        in_specs=[vmem],
-        out_specs=vmem,
+        in_specs=[anywhere],
+        out_specs=anywhere,
+        scratch_shapes=[pltpu.SemaphoreType.DMA(())],
         cost_estimate=pl.CostEstimate(flops=0, transcendentals=0, bytes_accessed=2 * block.size * 2),
     )(block)
 

time: 152 us -> 171 us (1.12)
  Pallas kernels: 150 us -> 169 us
    pallas_call x1, Pallas kernels: 1.97 us -> 21 us  [hand_over(): pl.pallas_call(hand_over_kernel, out_shape=jax.ShapeDtypeStruct(block.sha...]
where the time goes in v13:
time: 171 us; the launch traced here: 170 us
  Pallas kernels  169 us (99%)
    pallas_call x1, Pallas kernels, fused_attend(): pl.pallas_call(functools.partial(fused_kernel, frames, tiles), out_shape=...  148 us
    pallas_call x1, Pallas kernels, hand_over(): pl.pallas_call(hand_over_kernel, out_shape=jax.ShapeDtypeStruct(block.sha...  21 us

profile of v13, /device:TPU:224, one launch (start us, length us, event | category | flops | bytes accessed | tf_op | source)
XLA Modules:
  0.0 170.1 jit_solution(16175434544416520096)
XLA Ops:
  1.3 147.8 %shard_map.82.src_ref = bf16[64,5120]{1,0:T(8,128)(2,1)} custom-call(s32[1]{0:T(128)S(6)} %copy.9.step_ref, s32[1]{0:T(128)S(6)} %copy.10.fidx_ref, s32[9,40]{1,0:T(8,128)} %bitcast.8, s32[1,5]{1,0:T(1,128)} %hm_ref.1, f32[4,40]{1,0:T(4,128)} %sg_ref.1, bf16[64,5120]{1,0:T(8,128)(2,1)} %bitcast.5, bf16[64,5120]{1,0:T(8,128)(2,1)} %bitcast.6, ...), custom_call_target="tpu_custom_call" | custom-call | flops 4026531840 | bytes 14417920 | tf_op jit(solution)/shard_map/pallas_call | solution.py:279
  149.1 21.0 %shard_map.83 = bf16[64,5120]{1,0:T(8,128)(2,1)} custom-call(bf16[64,5120]{1,0:T(8,128)(2,1)} %shard_map.82.src_ref), custom_call_target="tpu_custom_call" | custom-call | bytes 1310720 | tf_op jit(solution)/shard_map/pallas_call | solution.py:321

commit v14 on v10

--- a/solution.py
+++ b/solution.py
@@ -15,7 +15,7 @@
 BLK = 4
 WIN = 5
 STEPS = 4
-CHUNK = 128
+CHUNK = 256
 
 NEG_BIG = -1e30
 MESH_ID = pl.DeviceIdType.MESH

time: 152 us -> 152 us (level)
  no operation moved by 1% of the time
where the time goes in v14:
time: 152 us
  Pallas kernels  151 us (99%)
    pallas_call x1, Pallas kernels, fused_attend(): pl.pallas_call(functools.partial(fused_kernel, frames, tiles), out_shape=...  149 us

profile of v14, /device:TPU:224, one launch (start us, length us, event | category | flops | bytes accessed | tf_op | source)
XLA Modules:
  0.0 152.3 jit_solution(7819888954610867085)
XLA Ops:
  1.3 149.0 %shard_map.82.src_ref = bf16[64,5120]{1,0:T(8,128)(2,1)} custom-call(s32[1]{0:T(128)S(6)} %copy.9.step_ref, s32[1]{0:T(128)S(6)} %copy.10.fidx_ref, s32[9,40]{1,0:T(8,128)} %bitcast.8, s32[1,5]{1,0:T(1,128)} %hm_ref.1, f32[4,40]{1,0:T(4,128)} %sg_ref.1, bf16[64,5120]{1,0:T(8,128)(2,1)} %bitcast.5, bf16[64,5120]{1,0:T(8,128)(2,1)} %bitcast.6, ...), custom_call_target="tpu_custom_call" | custom-call | flops 4026531840 | bytes 14417920 | tf_op jit(solution)/shard_map/pallas_call | solution.py:279
  150.3 2.0 %shard_map.83 = bf16[64,5120]{1,0:T(8,128)(2,1)} custom-call(bf16[64,5120]{1,0:T(8,128)(2,1)} %shard_map.82.src_ref), custom_call_target="tpu_custom_call" | custom-call | bytes 1310720 | tf_op jit(solution)/shard_map/pallas_call | solution.py:319

commit v15 on v10

--- a/solution.py
+++ b/solution.py
@@ -223,7 +223,7 @@
         peer = lax.rem(tile + offset, tiles)
         return pltpu.make_async_remote_copy(
             src_ref=fin.at[tokens_of(peer), :],
-            dst_ref=got_out.at[:, channels_of(tile)],
+            dst_ref=out_ref.at[:, channels_of(tile)],
             send_sem=piece_send.at[3, offset],
             recv_sem=piece_recv.at[3, tile],
             device_id=(me, peer),
@@ -234,14 +234,14 @@
         sender = lax.rem(tile + tiles - offset, tiles)
         return pltpu.make_async_remote_copy(
             src_ref=fin.at[tokens_of(tile), :],
-            dst_ref=got_out.at[:, channels_of(sender)],
+            dst_ref=out_ref.at[:, channels_of(sender)],
             send_sem=piece_send.at[3, offset],
             recv_sem=piece_recv.at[3, sender],
             device_id=(me, sender),
             device_id_type=MESH_ID,
         )
 
-    home = pltpu.make_async_copy(fin.at[tokens_of(tile), :], got_out.at[:, channels_of(tile)],
+    home = pltpu.make_async_copy(fin.at[tokens_of(tile), :], out_ref.at[:, channels_of(tile)],
                                  local_sem.at[3])
     home.start()
     for offset in range(1, tiles):
@@ -249,7 +249,6 @@
     home.wait()
     for offset in range(1, tiles):
         back_in(offset).wait_recv()
-    out_ref[...] = got_out[...]
 
     for which in range(3):
         for offset in range(1, tiles):

time: 152 us -> 152 us (level)
  no operation moved by 1% of the time
where the time goes in v15:
time: 152 us; the launch traced here: 151 us
  Pallas kernels  150 us (99%)
    pallas_call x1, Pallas kernels, fused_attend(): pl.pallas_call(functools.partial(fused_kernel, frames, tiles), out_shape=...  148 us

profile of v15, /device:TPU:224, one launch (start us, length us, event | category | flops | bytes accessed | tf_op | source)
XLA Modules:
  0.0 151.0 jit_solution(5355859071247224717)
XLA Ops:
  1.3 147.8 %shard_map.82.src_ref = bf16[64,5120]{1,0:T(8,128)(2,1)} custom-call(s32[1]{0:T(128)S(6)} %copy.9.step_ref, s32[1]{0:T(128)S(6)} %copy.10.fidx_ref, s32[9,40]{1,0:T(8,128)} %bitcast.8, s32[1,5]{1,0:T(1,128)} %hm_ref.1, f32[4,40]{1,0:T(4,128)} %sg_ref.1, bf16[64,5120]{1,0:T(8,128)(2,1)} %bitcast.5, bf16[64,5120]{1,0:T(8,128)(2,1)} %bitcast.6, ...), custom_call_target="tpu_custom_call" | custom-call | flops 4026531840 | bytes 14417920 | tf_op jit(solution)/shard_map/pallas_call | solution.py:278
  149.1 2.0 %shard_map.83 = bf16[64,5120]{1,0:T(8,128)(2,1)} custom-call(bf16[64,5120]{1,0:T(8,128)(2,1)} %shard_map.82.src_ref), custom_call_target="tpu_custom_call" | custom-call | bytes 1310720 | tf_op jit(solution)/shard_map/pallas_call | solution.py:318

commit v16 on v10

--- a/solution.py
+++ b/solution.py
@@ -120,12 +120,13 @@
         nearby = (row_step >= -1) & (row_step <= 1) & (across >= -1) & (across <= 1)
         code_scr[pl.ds(c * CHUNK, CHUNK), :] = jnp.where(nearby, (row_step + 1) * 3 + across + 1, 15)
 
-    def first_hop(p):
-        return pltpu.make_async_remote_copy(
-            src_ref=own_kv.at[:, tokens_of(p), :],
-            dst_ref=slots.at[0, :, tokens_of(p), :],
-            send_sem=hop_send.at[p],
-            recv_sem=hop_recv.at[p],
+    def hop(step, p):
+        source = own_kv if step == 0 else slots.at[step - 1]
+        return pltpu.make_async_remote_copy(
+            src_ref=source.at[:, tokens_of(p), :],
+            dst_ref=slots.at[step, :, tokens_of(p), :],
+            send_sem=hop_send.at[step, p],
+            recv_sem=hop_recv.at[step, p],
             device_id=(right, tile),
             device_id_type=MESH_ID,
         )
@@ -135,7 +136,7 @@
 
     @pl.when(me < frames - 1)
     def _():
-        first_hop(tile).start()
+        hop(0, tile).start()
 
     for offset in near_first:
         for which in range(2):
@@ -143,7 +144,7 @@
 
         @pl.when(me < frames - 1)
         def _():
-            first_hop(lax.rem(tile + tiles - offset, tiles)).start()
+            hop(0, lax.rem(tile + tiles - offset, tiles)).start()
 
     def copy_for(step):
         source = own_kv if step == 0 else slots.at[step - 1]
@@ -156,7 +157,6 @@
             device_id_type=MESH_ID,
         )
 
-    copies = [None] + [copy_for(step) for step in range(1, WIN)]
 
     m_scr[...] = jnp.full(m_scr.shape, NEG_BIG, jnp.float32)
     l_scr[...] = jnp.zeros(l_scr.shape, jnp.float32)
@@ -203,13 +203,15 @@
         def _():
             if step == 1:
                 for p in range(tiles):
-                    first_hop(p).wait_recv()
+                    hop(0, p).wait_recv()
             else:
-                copies[step - 1].wait_recv()
+                for p in range(tiles):
+                    hop(step - 1, p).wait_recv()
             if step < WIN:
                 @pl.when(me < frames - 1)
                 def _():
-                    copies[step].start()
+                    for p in range(tiles):
+                        hop(step, p).start()
             attend(slots.at[step - 1], usable(step))
 
     def finish(h, carry):
@@ -259,12 +261,13 @@
     for step in range(1, WIN):
         @pl.when((me < frames - 1) & (me >= step))
         def _():
-            copies[step].wait_send()
+            for p in range(tiles):
+                hop(step, p).wait_send()
 
     @pl.when(me < frames - 1)
     def _():
         for p in range(tiles):
-            first_hop(p).wait_send()
+            hop(0, p).wait_send()
 
 
 def fused_attend(frames, tiles, scalars, q, k, v):
@@ -296,8 +299,8 @@
             pltpu.SemaphoreType.DMA((4,)),
             pltpu.SemaphoreType.DMA((WIN,)),
             pltpu.SemaphoreType.DMA((WIN,)),
-            pltpu.SemaphoreType.DMA((tiles,)),
-            pltpu.SemaphoreType.DMA((tiles,)),
+            pltpu.SemaphoreType.DMA((WIN, tiles)),
+            pltpu.SemaphoreType.DMA((WIN, tiles)),
         ],
         compiler_params=pltpu.CompilerParams(
             collective_id=0, has_side_effects=True, vmem_limit_bytes=56 * 1024 * 1024

time: 152 us -> 152 us (level)
  no operation moved by 1% of the time
where the time goes in v16:
time: 152 us
  Pallas kernels  150 us (99%)
    pallas_call x1, Pallas kernels, fused_attend(): pl.pallas_call(functools.partial(fused_kernel, frames, tiles), out_shape=...  148 us

profile of v16, /device:TPU:224, one launch (start us, length us, event | category | flops | bytes accessed | tf_op | source)
XLA Modules:
  0.0 151.7 jit_solution(9020000773983229500)
XLA Ops:
  1.3 148.4 %shard_map.82.src_ref = bf16[64,5120]{1,0:T(8,128)(2,1)} custom-call(s32[1]{0:T(128)S(6)} %copy.9.step_ref, s32[1]{0:T(128)S(6)} %copy.10.fidx_ref, s32[9,40]{1,0:T(8,128)} %bitcast.8, s32[1,5]{1,0:T(1,128)} %hm_ref.1, f32[4,40]{1,0:T(4,128)} %sg_ref.1, bf16[64,5120]{1,0:T(8,128)(2,1)} %bitcast.5, bf16[64,5120]{1,0:T(8,128)(2,1)} %bitcast.6, ...), custom_call_target="tpu_custom_call" | custom-call | flops 4026531840 | bytes 14417920 | tf_op jit(solution)/shard_map/pallas_call | solution.py:282
  149.7 2.0 %shard_map.83 = bf16[64,5120]{1,0:T(8,128)(2,1)} custom-call(bf16[64,5120]{1,0:T(8,128)(2,1)} %shard_map.82.src_ref), custom_call_target="tpu_custom_call" | custom-call | bytes 1310720 | tf_op jit(solution)/shard_map/pallas_call | solution.py:322
